TPU v7x, 256 devices: a whole 4x4x8 slice. The times are simulated.
256 devices in a mesh: refl: 8 (over z_hi, y), slab: 32 (over z_lo, x, core).
Axes of the slice: x: 4, y: 4, z: 8 (z_hi: 2, z_lo: 4; z = z_hi * 4 + z_lo), core: 2. Of those that a mesh axis runs over, the one named last changes fastest.
Arguments:
- amplitude: float32 [128, 128, 128], P('slab', 'refl'), may hold values from 1 to 3
- displacement: float32 [3, 128, 128, 128], P(None, 'slab', 'refl'), may hold values from -12 to 12
- support: int32 [128, 128, 128], P('slab'), may hold values from 0 to 1, as said below
- miller: int32 [8, 3], P('refl'), may hold values from -2 to 2, as said below
- shift_kz: int32 [8], P('refl'), may hold values from 0 to 255
- intensity: float32 [8, 256, 256, 256], P('refl', None, 'slab'), may hold values from 0.02 to 0.5
Outputs:
- grad_amplitude: float32 [128, 128, 128], P('slab', 'refl')
- grad_displacement: float32 [3, 128, 128, 128], P(None, 'slab', 'refl')
Inputs may be any that keep to these rules, and one draw needn't show every extreme that they name: 1 inside the object's support, 0 outside. `miller`: no index is zero.
All inputs are finite; a program needn't handle non-finite values.
Results may differ from a plain program's by a relative error of at most 0.0003.
Values sent between devices are 32-bit elements; how exact they have to be, the bound alone decides.
A program may use at most 64 MiB of HBM per device.

v0:
```python
import jax
import jax.numpy as jnp
from jax import lax
from jax.sharding import PartitionSpec as P

STRAIN_WEIGHT = 0.05
EDGE_WEIGHT = 0.05


def cut_along(x, dim, count):
    before, after = (x.shape[:dim], x.shape[dim + 1 :])
    return jnp.moveaxis(x.reshape(*before, count, -1, *after), dim, 0)


def extended_2(x, sides, width):
    edges = {}
    for axis, dim in sides:
        count, length = (lax.axis_size(axis), x.shape[dim])
        up = [(i, (i + 1) % count) for i in range(count - 1)]
        last = lax.slice_in_dim(x, length - width, length, axis=dim)
        leading = lax.slice_in_dim(x, 0, width, axis=dim)
        edges[dim] = (
            lax.ppermute(last, axis, up),
            lax.ppermute(leading, axis, [(b, a) for a, b in up]),
        )
    done = []
    for _, dim in sides:
        low, high = edges[dim]
        around = [(width, width) if d in done else (0, 0) for d in range(x.ndim)]
        x = jnp.concatenate([jnp.pad(low, around), x, jnp.pad(high, around)], axis=dim)
        done.append(dim)
    return x


def tables(freqs, places, length):
    product = freqs[:, None] * places[None, :] % length
    angle = 2.0 * jnp.pi / length * product.astype(jnp.float32)
    factor = length ** (-0.5)
    return (jnp.cos(angle) * factor, jnp.sin(angle) * factor)


def transform(parts, matrices, pattern, forward):
    cosine, sine = matrices

    def multiply(matrix, operand):
        return jnp.einsum(
            pattern,
            operand,
            matrix,
            precision=lax.Precision.HIGH,
            preferred_element_type=jnp.float32,
        )

    cos_real = multiply(cosine, parts[0])
    cos_imag = multiply(cosine, parts[1])
    sin_real = multiply(sine, parts[0])
    sin_imag = multiply(sine, parts[1])
    if forward:
        return (cos_real + sin_imag, cos_imag - sin_real)
    return (cos_real - sin_imag, cos_imag + sin_real)


def everyone(x, axis):
    count = lax.axis_size(axis)
    spread = jnp.broadcast_to(x[None], (count, *x.shape))
    return lax.all_to_all(spread, axis, 0, 0, tiled=True)


def body(amplitude, displacement, support, miller, shift_kz, intensity):
    owned = amplitude.shape[1]
    edge = amplitude.shape[2]
    grid = 2 * edge
    refl_index = lax.axis_index("refl")
    mask = support.astype(jnp.float32)
    mask_own = lax.dynamic_slice_in_dim(mask, refl_index * owned, owned, 1)
    fields = jnp.concatenate([(mask_own * amplitude)[None], displacement], axis=0)
    whole = everyone(fields, "refl")
    weight, d0, d1, d2 = [
        jnp.moveaxis(whole[:, c], 0, 1).reshape(amplitude.shape[0], edge, edge) for c in range(4)
    ]
    millers = everyone(miller[0].astype(jnp.float32), "refl")
    miller_row = miller[0].astype(jnp.float32)
    every = jnp.arange(grid, dtype=jnp.int32)
    inner = jnp.arange(edge, dtype=jnp.int32)
    turn = (shift_kz[0] * inner % grid).astype(jnp.float32) * (2.0 * jnp.pi / grid)
    phase = miller_row[0] * d0 + miller_row[1] * d1 + miller_row[2] * d2 + turn
    cosine = jnp.cos(phase)
    sine = jnp.sin(phase)
    target = (weight * cosine, weight * sine)
    half_mats = tables(every, inner, grid)
    why_done = transform(target, half_mats, "anz,kn->akz", True)
    both = jnp.stack(why_done)
    moved = lax.all_to_all(both, "slab", 2, 1, tiled=True)
    zed_done = transform(moved, half_mats, "xyn,kn->xyk", True)
    spectrum = transform(zed_done, half_mats, "nyk,xn->xyk", True)
    power = spectrum[0] * spectrum[0] + spectrum[1] * spectrum[1]
    excess = 4.0 * (power - intensity[0])
    residual = (excess * spectrum[0], excess * spectrum[1])
    back_x = transform(residual, half_mats, "xyk,xn->nyk", False)
    back_z = transform(back_x, half_mats, "xyk,kn->xyn", False)
    returned = lax.all_to_all(jnp.stack(back_z), "slab", 1, 2, tiled=True)
    adjoint = transform(returned, half_mats, "akz,kn->anz", False)
    along = adjoint[0] * cosine + adjoint[1] * sine
    across = weight * (adjoint[1] * cosine - adjoint[0] * sine)
    pair = jnp.stack([along, across])
    parts = lax.all_to_all(cut_along(pair, 2, lax.axis_size("refl")), "refl", 0, 0, tiled=True)
    summed_amp = mask_own * jnp.sum(parts[:, 0], axis=0)
    summed_disp = jnp.sum(millers[:, :, None, None, None] * parts[:, 1][:, None], axis=0)
    extended = extended_2(fields, (("refl", 2), ("slab", 1)), 1)
    extended = jnp.pad(extended, ((0, 0), (0, 0), (0, 0), (1, 1)))
    centre = extended[:, 1:-1, 1:-1, 1:-1]
    beside = extended[:, 2:, 1:-1, 1:-1] + extended[:, :-2, 1:-1, 1:-1]
    beside = beside + extended[:, 1:-1, 2:, 1:-1] + extended[:, 1:-1, :-2, 1:-1]
    beside = beside + extended[:, 1:-1, 1:-1, 2:] + extended[:, 1:-1, 1:-1, :-2]
    lapped = 6.0 * centre - beside
    amp_total = summed_amp + 2.0 * EDGE_WEIGHT * mask_own * lapped[0]
    disp_total = summed_disp + 2.0 * STRAIN_WEIGHT * lapped[1:]
    return (amp_total, disp_total)


def solution(mesh):
    placed = (
        P("slab", "refl", None),
        P(None, "slab", "refl", None),
        P("slab", None, None),
        P("refl", None),
        P("refl"),
        P("refl", None, "slab", None),
    )
    return jax.shard_map(
        body,
        mesh=mesh,
        in_specs=placed,
        out_specs=(P("slab", "refl", None), P(None, "slab", "refl", None)),
        check_vma=False,
    )
```

profile of v0, /device:TPU:1, one launch (start us, length us, event | category | flops | bytes accessed | tf_op | source)
XLA Modules:
  0.0 187.6 jit_solution(2971703182053405410)
XLA Ops:
  0.6 0.0 copy-start.2
  0.6 0.8 multiply_bitcast_fusion
  1.4 0.9 pad_maximum_fusion.3
  2.3 1.1 broadcast_in_dim.7
  3.4 11.6 %all-to-all-start = ((f32[8,4,4,16,128]{4,3,2,1,0:T(8,128)}), f32[8,4,4,16,128]{4,3,2,1,0:T(8,128)S(1)}, u32[]{:S(2)}, u32[]{:S(2)}) async-start(f32[8,4,4,16,128]{4,3,2,1,0:T(8,128)} %broadcast_in_dim.7), calls=%async_computation | async-start | bytes 2097152 | tf_op jit(solution)/shard_map/all_to_all | solution.py:66
  15.8 0.6 fusion.196
  16.4 17.5 %all-to-all-done = f32[8,4,4,16,128]{4,3,2,1,0:T(8,128)S(1)} async-done(((f32[8,4,4,16,128]{4,3,2,1,0:T(8,128)}), f32[8,4,4,16,128]{4,3,2,1,0:T(8,128)S(1)}, u32[]{:S(2)}, u32[]{:S(2)}) %all-to-all-start) | async-done | bytes 1048608 | tf_op jit(solution)/shard_map/all_to_all | solution.py:66
  33.8 2.0 %fusion.13 = (f32[4,8,16,128]{3,2,0,1:T(8,128)S(1)}, f32[4,8,16,128]{3,2,0,1:T(8,128)S(1)}) fusion(f32[8,4,4,16,128]{4,3,2,1,0:T(8,128)S(1)} %all-to-all-done, f32[]{:T(128)} %bitcast.9, f32[]{:T(128)} %bitcast.8, f32[]{:T(128)} %bitcast.7), kind=kLoop, calls=%fused_computation.50 | loop fusion | flops 327680 | bytes 1572876 | tf_op jit(solution)/shard_map/add | solution.py:86
  35.9 1.0 bitcast_multiply_fusion.2
  36.9 0.9 fusion.48
  37.8 0.9 fusion.46
  38.8 0.9 fusion.6
  39.7 0.9 fusion.5
  40.6 0.1 pad_maximum_fusion
  40.6 0.7 copy.64
  41.3 43.0 %all_to_all.46 = f32[2,4,256,128]{3,1,0,2:T(4,128)S(1)} all-to-all(f32[2,4,256,128]{3,1,0,2:T(4,128)S(1)} %copy.64), channel_id=1, replica_groups=mesh['refl'=8,'slab'=32] {'slab'}, dimensions={2} | all-to-all | bytes 2097152 | tf_op jit(solution)/shard_map/all_to_all | solution.py:93
  84.3 0.3 copy.132
  84.6 0.1 fusion.195
  84.7 1.1 fusion.44
  85.8 1.1 fusion.42
  86.9 1.1 convolution_add_fusion.2
  87.9 1.5 fusion.50
  89.5 1.1 convolution_subtract_fusion.2
  90.6 1.5 fusion.40
  92.1 1.5 convolution_add_fusion
  93.6 0.0 copy-start
  93.7 1.5 convolution_subtract_fusion
  95.2 0.0 copy-done
  95.2 2.1 %fusion.56 = f32[128,8,256]{2,0,1:T(8,128)S(1)} fusion(f32[256,8,256]{2,0,1:T(8,128)S(1)} %convolution_add_fusion, f32[1,256,8,256]{3,2,1,0:T(8,128)S(1)} %copy-done, f32[256,8,256]{2,0,1:T(8,128)S(1)} %convolution_subtract_fusion), kind=kOutput, calls=%fused_computation.122 | convolution fusion | flops 406290432 | bytes 7340032 | tf_op jit(solution)/shard_map/xyk,xn->nyk/dot_general | solution.py:46
  97.3 1.9 fusion.54
  99.2 1.9 convolution_subtract_fusion.1
  101.1 1.1 fusion.38
  102.2 1.9 %convolution_add_fusion.1 = f32[128,8,256]{2,0,1:T(8,128)S(1)} fusion(f32[128,8,256]{2,0,1:T(8,128)S(1)} %fusion.54, f32[256,8,256]{2,0,1:T(8,128)S(1)} %convolution_add_fusion, f32[1,256,8,256]{3,2,1,0:T(8,128)S(1)} %copy-done, f32[256,8,256]{2,0,1:T(8,128)S(1)} %convolution_subtract_fusion), kind=kOutput, calls=%fused_computation.6 | convolution fusion | flops 406552576 | bytes 8388608 | tf_op jit(solution)/shard_map/xyk,xn->nyk/dot_general | solution.py:46
  104.1 1.1 fusion.36
  105.1 1.1 fusion.3
  106.2 1.1 fusion.4
  107.3 0.1 pad_maximum_fusion.1
  107.4 0.6 copy.79
  108.0 31.6 %all_to_all.47 = f32[2,128,8,128]{3,2,0,1:T(8,128)S(1)} all-to-all(f32[2,128,8,128]{3,2,0,1:T(8,128)S(1)} %copy.79), channel_id=1, replica_groups=mesh['refl'=8,'slab'=32] {'slab'}, dimensions={1} | all-to-all | bytes 2097152 | tf_op jit(solution)/shard_map/all_to_all | solution.py:101
  139.6 0.1 copy.131
  139.7 0.8 fusion.10
  140.5 0.8 fusion.11
  141.3 0.8 fusion.8
  142.1 0.0 copy-start.1
  142.1 1.7 multiply_add_fusion
  143.7 0.9 copy_bitcast_fusion.2
  144.6 3.7 %all-to-all-start.3 = ((f32[8,2,4,16,128]{4,3,2,1,0:T(8,128)}), f32[8,2,4,16,128]{4,3,2,1,0:T(8,128)S(1)}, u32[]{:S(2)}, u32[]{:S(2)}) async-start(f32[8,2,4,16,128]{4,3,2,1,0:T(8,128)} %copy_bitcast_fusion.2), calls=%async_computation.3 | async-start | bytes 1048576 | tf_op jit(solution)/shard_map/all_to_all | solution.py:106
  148.3 2.1 %collective-permute-start.2 = (f32[4,1,16,128]{3,2,1,0:T(8,128)S(1)}, f32[4,1,16,128]{3,2,1,0:T(8,128)S(1)}, u32[]{:S(2)}, u32[]{:S(2)}) collective-permute-start(f32[4,1,16,128]{3,2,1,0:T(8,128)S(1)} %get-tuple-element.15), channel_id=1, source_target_pairs={{1,0},{2,1},{3,2},{4,3},{5,4},{6,5},{7,6},{8,7},{9,8},{10,9},{11,1... | collective-permute-start | bytes 98312 | tf_op jit(solution)/shard_map/ppermute | solution.py:24
  150.4 3.5 %collective-permute-start.3 = (f32[4,1,16,128]{3,2,1,0:T(8,128)S(1)}, f32[4,1,16,128]{3,2,1,0:T(8,128)S(1)}, u32[]{:S(2)}, u32[]{:S(2)}) collective-permute-start(f32[4,1,16,128]{3,2,1,0:T(8,128)S(1)} %get-tuple-element.14), channel_id=1, source_target_pairs={{0,1},{1,2},{2,3},{3,4},{4,5},{5,6},{6,7},{7,8},{8,9},{9,10},{10,1... | collective-permute-start | bytes 98312 | tf_op jit(solution)/shard_map/ppermute | solution.py:23
  153.9 3.4 %collective-permute-start = (f32[4,4,1,128]{3,2,1,0:T(1,128)S(1)}, f32[4,4,1,128]{3,2,1,0:T(1,128)S(1)}, u32[]{:S(2)}, u32[]{:S(2)}) collective-permute-start(f32[4,4,1,128]{3,2,1,0:T(1,128)S(1)} %get-tuple-element.12), channel_id=1, source_target_pairs={{0,32},{32,64},{64,96},{96,128},{128,160},{160,192},{192,224},{1,3... | collective-permute-start | bytes 24584 | tf_op jit(solution)/shard_map/ppermute | solution.py:23
  157.3 1.3 collective-permute-start.1
  158.6 0.0 collective-permute-done.2
  158.6 0.0 collective-permute-done.3
  158.6 0.0 collective-permute-done
  158.7 3.4 %collective-permute-done.1 = f32[4,4,1,128]{3,2,1,0:T(1,128)S(1)} collective-permute-done((f32[4,4,1,128]{3,2,1,0:T(1,128)S(1)}, f32[4,4,1,128]{3,2,1,0:T(1,128)S(1)}, u32[]{:S(2)}, u32[]{:S(2)}) %collective-permute-start.1) | collective-permute-done | bytes 8224 | tf_op jit(solution)/shard_map/ppermute | solution.py:24
  162.0 0.3 select_maximum_fusion
  162.3 0.1 fusion.20
  162.4 0.0 all-to-all-done.3
  162.4 0.6 broadcast_in_dim.8
  163.0 13.6 %all-to-all-start.4 = ((f32[8,1,3]{2,1,0:T(1,128)}), f32[8,1,3]{2,1,0:T(1,128)S(1)}, u32[]{:S(2)}, u32[]{:S(2)}) async-start(f32[8,1,3]{2,1,0:T(1,128)} %broadcast_in_dim.8), calls=%async_computation.4 | async-start | bytes 8192 | tf_op jit(solution)/shard_map/all_to_all | solution.py:66
  176.6 8.8 %all-to-all-done.4 = f32[8,1,3]{2,1,0:T(1,128)S(1)} async-done(((f32[8,1,3]{2,1,0:T(1,128)}), f32[8,1,3]{2,1,0:T(1,128)S(1)}, u32[]{:S(2)}, u32[]{:S(2)}) %all-to-all-start.4) | async-done | bytes 128 | tf_op jit(solution)/shard_map/all_to_all | solution.py:66
  185.4 0.1 multiply_reduce_fusion
  185.6 0.7 fusion.61
  186.2 1.4 fusion.65
  (11 shorter events, 0.1 us)
Async XLA Ops:
  0.6 15.1 %copy-start.2 = (s32[1,3]{1,0:T(1,128)S(1)}, s32[1,3]{1,0:T(1,128)}, u32[]{:S(2)}) copy-start(s32[1,3]{1,0:T(1,128)} %param.9) | copy-start | bytes 40
  3.4 30.4 %all-to-all-start = ((f32[8,4,4,16,128]{4,3,2,1,0:T(8,128)}), f32[8,4,4,16,128]{4,3,2,1,0:T(8,128)S(1)}, u32[]{:S(2)}, u32[]{:S(2)}) async-start(f32[8,4,4,16,128]{4,3,2,1,0:T(8,128)} %broadcast_in_dim.7), calls=%async_computation | async-start | bytes 2097152 | tf_op jit(solution)/shard_map/all_to_all | solution.py:66
  93.6 1.6 copy-start
  142.1 6.2 %copy-start.1 = (f32[3,4,16,128]{3,2,1,0:T(8,128)S(1)}, f32[3,4,16,128]{3,2,1,0:T(8,128)}, u32[]{:S(2)}) copy-start(f32[3,4,16,128]{3,2,1,0:T(8,128)} %param.7) | copy-start | bytes 294916
  144.6 17.8 %all-to-all-start.3 = ((f32[8,2,4,16,128]{4,3,2,1,0:T(8,128)}), f32[8,2,4,16,128]{4,3,2,1,0:T(8,128)S(1)}, u32[]{:S(2)}, u32[]{:S(2)}) async-start(f32[8,2,4,16,128]{4,3,2,1,0:T(8,128)} %copy_bitcast_fusion.2), calls=%async_computation.3 | async-start | bytes 1048576 | tf_op jit(solution)/shard_map/all_to_all | solution.py:106
  148.3 10.3 %collective-permute-start.2 = (f32[4,1,16,128]{3,2,1,0:T(8,128)S(1)}, f32[4,1,16,128]{3,2,1,0:T(8,128)S(1)}, u32[]{:S(2)}, u32[]{:S(2)}) collective-permute-start(f32[4,1,16,128]{3,2,1,0:T(8,128)S(1)} %get-tuple-element.15), channel_id=1, source_target_pairs={{1,0},{2,1},{3,2},{4,3},{5,4},{6,5},{7,6},{8,7},{9,8},{10,9},{11,1... | collective-permute-start | bytes 98312 | tf_op jit(solution)/shard_map/ppermute | solution.py:24
  150.4 8.2 %collective-permute-start.3 = (f32[4,1,16,128]{3,2,1,0:T(8,128)S(1)}, f32[4,1,16,128]{3,2,1,0:T(8,128)S(1)}, u32[]{:S(2)}, u32[]{:S(2)}) collective-permute-start(f32[4,1,16,128]{3,2,1,0:T(8,128)S(1)} %get-tuple-element.14), channel_id=1, source_target_pairs={{0,1},{1,2},{2,3},{3,4},{4,5},{5,6},{6,7},{7,8},{8,9},{9,10},{10,1... | collective-permute-start | bytes 98312 | tf_op jit(solution)/shard_map/ppermute | solution.py:23
  153.9 4.7 %collective-permute-start = (f32[4,4,1,128]{3,2,1,0:T(1,128)S(1)}, f32[4,4,1,128]{3,2,1,0:T(1,128)S(1)}, u32[]{:S(2)}, u32[]{:S(2)}) collective-permute-start(f32[4,4,1,128]{3,2,1,0:T(1,128)S(1)} %get-tuple-element.12), channel_id=1, source_target_pairs={{0,32},{32,64},{64,96},{96,128},{128,160},{160,192},{192,224},{1,3... | collective-permute-start | bytes 24584 | tf_op jit(solution)/shard_map/ppermute | solution.py:23
  157.3 4.7 %collective-permute-start.1 = (f32[4,4,1,128]{3,2,1,0:T(1,128)S(1)}, f32[4,4,1,128]{3,2,1,0:T(1,128)S(1)}, u32[]{:S(2)}, u32[]{:S(2)}) collective-permute-start(f32[4,4,1,128]{3,2,1,0:T(1,128)S(1)} %get-tuple-element.13), channel_id=1, source_target_pairs={{32,0},{64,32},{96,64},{128,96},{160,128},{192,160},{224,192},{33,... | collective-permute-start | bytes 24584 | tf_op jit(solution)/shard_map/ppermute | solution.py:24
  163.0 22.4 %all-to-all-start.4 = ((f32[8,1,3]{2,1,0:T(1,128)}), f32[8,1,3]{2,1,0:T(1,128)S(1)}, u32[]{:S(2)}, u32[]{:S(2)}) async-start(f32[8,1,3]{2,1,0:T(1,128)} %broadcast_in_dim.8), calls=%async_computation.4 | async-start | bytes 8192 | tf_op jit(solution)/shard_map/all_to_all | solution.py:66
where the time goes:
time: 190 us; the launch traced here: 188 us
  blocking collectives  74.6 us (39%)
  starting transfers between devices  39.1 us (21%)
  matrix products  30.1 us (16%)
  waiting for transfers between devices  29.7 us (16%)
  other arithmetic  8.34 us (4%)
  local copies, waits for them, and re-layouts  4.1 us (2%)
    all_to_all x1, blocking collectives, body(): moved = lax.all_to_all(both, 'slab', 2, 1, tiled=True)  43 us
    all_to_all x1, blocking collectives, body(): returned = lax.all_to_all(jnp.stack(back_z), 'slab', 1, 2, tiled=True)  31.6 us
    dot_general x24, matrix products, multiply(): jnp.einsum(pattern, operand, matrix, precision=lax.Precision.HIGH, prefer...  30.1 us
    all_to_all x2, waiting for transfers between devices, everyone(): return lax.all_to_all(spread, axis, 0, 0, tiled=True)  26.3 us
    all_to_all x2, starting transfers between devices, everyone(): return lax.all_to_all(spread, axis, 0, 0, tiled=True)  25.2 us
    ppermute x2, starting transfers between devices, extended_2(): lax.ppermute(last, axis, up)  6.84 us
  transfers between devices with their start and end apart: 7, of which 3 were waited for; matrix products, arithmetic and copies ran while one was open for 1% of the time, Pallas kernels for 0%

commit v1 on v0

v1 whole, which is shorter than its diff:
```python
import math

import jax
import jax.numpy as jnp
from jax import lax
from jax.experimental import pallas as pl
from jax.experimental.pallas import tpu as pltpu
from jax.sharding import PartitionSpec as P

MESH = pl.DeviceIdType.MESH
F32 = jnp.float32
BF16 = jnp.bfloat16
STRAIN_WEIGHT = 0.05
EDGE_WEIGHT = 0.05
SLABS = 32
ROWS = 4
HALF = SLABS * 32


def sine_turns(v):
    w = v * v
    total = jnp.full_like(v, -((2 * math.pi) ** 11) / math.factorial(11))
    for power in (9, 7, 5, 3, 1):
        sign = 1.0 if power % 4 == 1 else -1.0
        total = total * w + sign * (2 * math.pi) ** power / math.factorial(power)
    return total * v


def cos_sin_turns(t):
    t = t - jnp.floor(t + 0.5)
    size = jnp.abs(t)
    cosine = sine_turns(0.25 - size)
    sine = sine_turns(0.25 - jnp.abs(size - 0.25))
    return cosine, jnp.where(t < 0.0, -sine, sine)


def split(x):
    high = x.astype(BF16)
    low = (x - high.astype(F32)).astype(BF16)
    return high, low


def stacked(x):
    high, low = split(x)
    return jnp.concatenate([high, low, high], axis=0)


def abreast(x):
    high, low = split(x)
    return jnp.concatenate([high, low, high], axis=1)


def dot(a, b):
    return jnp.dot(a, b, preferred_element_type=F32)


def freq_y(i):
    return 8 * ((i >> 1) & 31) + 4 * (i >> 8) + ((i >> 6) & 3), i & 1


def freq_plain(i):
    return i & 255, i >> 8


def place_plain(i):
    return i & 127, i >> 7


def place_x(i):
    return 4 * (i & 31) + ((i >> 5) & 3), i >> 7


def fill_table(ref, shape, row_is_freq, freq, place, on_left):
    rows, cols = shape
    chunk = 32

    def step(j, carry):
        start = pl.multiple_of(j * chunk, chunk)
        row = lax.broadcasted_iota(jnp.int32, (chunk, cols), 0) + start
        col = lax.broadcasted_iota(jnp.int32, (chunk, cols), 1)
        if row_is_freq:
            k, kc = freq(row)
            n, nc = place(col)
        else:
            k, kc = freq(col)
            n, nc = place(row)
        turns = ((k * n + 64 * (kc - nc) + 128) & 255) - 128
        t = turns.astype(F32) * (1.0 / 256.0)
        high, low = split(sine_turns(0.25 - jnp.abs(t)) * (1.0 / 16.0))
        if on_left:
            ref[pl.ds(start, chunk), 0:cols] = high
            ref[pl.ds(start, chunk), cols : 2 * cols] = high
            ref[pl.ds(start, chunk), 2 * cols : 3 * cols] = low
        else:
            ref[pl.ds(start, chunk), :] = high
            ref[pl.ds(pl.multiple_of(rows + start, chunk), chunk), :] = high
            ref[pl.ds(pl.multiple_of(2 * rows + start, chunk), chunk), :] = low
        return carry

    lax.fori_loop(0, rows // chunk, step, 0)


def kernel(
    amp_ref, disp_ref, sup_hbm, miller_ref, shift_ref, int_hbm,
    amp_out, disp_out,
    sup, inten, own, mate, mill, ey_send, ey_recv, ex_recv, trig, obj, obj_all, bcat,
    fwd_send, fwd_recv, back_send, back_recv, ydone, ydone_all, part, part_recv,
    y_fwd, y_back, x_fwd, x_back, z_fwd, z_back,
    load_sem, mate_sem, mill_sem, edge_sem, peer_sem, peer_back_sem, slab_sem, slab_back_sem, part_sem,
):
    refl = lax.axis_index("refl")
    me = lax.axis_index("slab")
    zh = refl // 4
    yy = lax.rem(refl, 4)
    mate_id = lax.rem(refl + 4, 8)

    def peer_of(t):
        return zh * 4 + lax.rem(yy + t, 4)

    sup_copy = pltpu.make_async_copy(
        sup_hbm.at[:, pl.ds(pl.multiple_of(refl * 16, 16), 16), :], sup, load_sem.at[0]
    )
    sup_copy.start()
    int_copies = [
        pltpu.make_async_copy(int_hbm.at[:, pl.ds(128 * j, 128)], inten.at[j], load_sem.at[1 + j])
        for j in range(2)
    ]
    for copy in int_copies:
        copy.start()

    barrier = pltpu.get_barrier_semaphore()

    def greet_slab(j, carry):
        pl.semaphore_signal(
            barrier, inc=1, device_id={"slab": lax.rem(me + j, SLABS)}, device_id_type=MESH
        )
        return carry

    def greet_refl(j, carry):
        pl.semaphore_signal(
            barrier, inc=1, device_id={"refl": lax.rem(refl + j, 8)}, device_id_type=MESH
        )
        return carry

    lax.fori_loop(1, 8, greet_refl, 0)
    lax.fori_loop(1, SLABS, greet_slab, 0)

    own[1:4] = disp_ref[...]
    lane_row = lax.broadcasted_iota(jnp.int32, (8, 128), 0)
    tile = jnp.where(
        lane_row == 0,
        miller_ref[0, 0].astype(F32),
        jnp.where(
            lane_row == 1,
            miller_ref[0, 1].astype(F32),
            jnp.where(lane_row == 2, miller_ref[0, 2].astype(F32), shift_ref[0].astype(F32)),
        ),
    )
    mill[yy] = tile
    sup_copy.wait()
    mask = sup[...].astype(F32)
    own[0] = mask * amp_ref[...]
    for f in range(4):
        for x in range(ROWS):
            at = f * 4 + x
            ey_send[0, at : at + 1, :] = own[f, x, 0:1, :]
            ey_send[1, at : at + 1, :] = own[f, x, 15:16, :]

    pl.semaphore_wait(barrier, 38)

    def remote(src, dst, sems, axis, target):
        return pltpu.make_async_remote_copy(
            src_ref=src,
            dst_ref=dst,
            send_sem=sems.at[0],
            recv_sem=sems.at[1],
            device_id={axis: target},
            device_id_type=MESH,
        )

    mate_copy = remote(own, mate, mate_sem, "refl", mate_id)
    mate_copy.start()
    mill_copies = [
        remote(mill.at[yy], mill.at[yy], mill_sem.at[t], "refl", peer_of(t)) for t in (1, 2, 3)
    ]
    for copy in mill_copies:
        copy.start()

    has = (refl > 0, refl < 7, me > 0, me < SLABS - 1)
    down_y = remote(ey_send.at[0], ey_recv.at[1], edge_sem.at[0], "refl", lax.rem(refl + 7, 8))
    up_y = remote(ey_send.at[1], ey_recv.at[0], edge_sem.at[1], "refl", lax.rem(refl + 1, 8))
    down_x = remote(own.at[:, 0], ex_recv.at[1], edge_sem.at[2], "slab", lax.rem(me + SLABS - 1, SLABS))
    up_x = remote(own.at[:, 3], ex_recv.at[0], edge_sem.at[3], "slab", lax.rem(me + 1, SLABS))
    edges = (down_y, up_y, down_x, up_x)
    for there, copy in zip(has, edges):
        pl.when(there)(copy.start)

    def nothing(ref, at):
        def fill():
            ref[at] = jnp.zeros(ref.shape[1:], F32)
        return fill

    for there, ref, at in zip(has, (ey_recv, ey_recv, ex_recv, ex_recv), (0, 1, 0, 1)):
        pl.when(jnp.logical_not(there))(nothing(ref, at))

    def place_y(i):
        side = ((i >> 4) & 1) + zh
        return ((side & 1) * 4 + (i >> 6)) * 16 + (i & 15), (i >> 5) & 1

    fill_table(y_fwd, (512, 256), True, freq_y, place_y, True)
    fill_table(y_back, (256, 512), False, freq_y, place_y, True)
    fill_table(x_fwd, (512, 256), True, freq_plain, place_x, True)
    fill_table(x_back, (256, 512), False, freq_plain, place_x, True)
    fill_table(z_fwd, (256, 512), False, freq_plain, place_plain, False)
    fill_table(z_back, (512, 256), True, freq_plain, place_plain, False)

    for t in (1, 2, 3):
        remote(mill.at[yy], mill.at[yy], mill_sem.at[t], "refl", peer_of(t)).wait_recv()
    mate_copy.wait_recv()
    lane = lax.broadcasted_iota(jnp.int32, (1, 1, 128), 2).astype(F32)

    def objects(t, store):
        coef = mill[lax.rem(yy + t, 4)]
        m0, m1, m2, s = [coef[j : j + 1][None] for j in range(4)]
        turn = s * lane * (1.0 / 256.0)
        turn = turn - jnp.floor(turn)
        for b, fields in enumerate((own, mate)):
            phase = m0 * fields[1] + m1 * fields[2] + m2 * fields[3]
            cosine, sine = cos_sin_turns(phase * (1.0 / (2 * math.pi)) + turn)
            trig[t, 0, b] = cosine
            trig[t, 1, b] = sine
            weight = fields[0]
            store(0, b, weight * cosine)
            store(1, b, weight * sine)

    def keep(t):
        def store(c, b, value):
            obj[t, c, b] = value
        return store

    def keep_own(c, b, value):
        obj_all[yy, c, b] = value

    obj_copies = {}
    for t in (2, 1, 3):
        objects(t, keep(t))
        obj_copies[t] = remote(obj.at[t], obj_all.at[yy], peer_sem.at[t], "refl", peer_of(t))
        obj_copies[t].start()
    objects(0, keep_own)
    for t in (2, 1, 3):
        obj_copies[t].wait_recv()

    for pair in range(2):
        columns = [
            obj_all[:, :, :, 2 * pair + j].reshape(256, 128) for j in range(2)
        ]
        bcat[pair] = stacked(jnp.concatenate(columns, axis=1))

    def slab_sends(src, dst, sems, h):
        def send(j, carry):
            to = lax.rem(me + j, SLABS)
            pltpu.make_async_remote_copy(
                src_ref=src.at[h, pl.ds(pl.multiple_of(to * 32, 32), 32)],
                dst_ref=dst.at[h, pl.ds(pl.multiple_of(me * 32, 32), 32)],
                send_sem=sems.at[0, h],
                recv_sem=sems.at[1, h],
                device_id={"slab": to},
                device_id_type=MESH,
            ).start()
            return carry

        lax.fori_loop(16, SLABS, send, 0)
        lax.fori_loop(1, 16, send, 0)
        mine = pl.ds(pl.multiple_of(me * 32, 32), 32)
        pltpu.make_async_copy(src.at[h, mine], dst.at[h, mine], sems.at[1, h]).start()

    def wait_sent(src, dst, sems, h):
        most = pl.ds(0, HALF - 32)
        pltpu.make_async_copy(src.at[h, most], dst.at[h, most], sems.at[0, h]).wait()

    def wait_arrived(dst, sems, h):
        pltpu.make_async_copy(dst.at[h], dst.at[h], sems.at[1, h]).wait()

    for h in range(2):
        for pair in range(2):
            out = dot(y_fwd[256 * h : 256 * (h + 1), :], bcat[pair])
            for k in range(4):
                for j in range(2):
                    fwd_send[h, pl.ds((2 * pair + j) * 4 + k, 64, stride=16), :] = out[
                        64 * k : 64 * (k + 1), 128 * j : 128 * (j + 1)
                    ]
        slab_sends(fwd_send, fwd_recv, slab_sem, h)

    for copy in int_copies:
        copy.wait()

    for h in range(2):
        wait_arrived(fwd_recv, slab_sem, h)

        def row(k, carry):
            sides = [
                jnp.concatenate(
                    [
                        fwd_recv[h, pl.ds(c * 16 + x * 4 + k, 32, stride=32), :]
                        for x in range(ROWS)
                    ],
                    axis=0,
                )
                for c in range(2)
            ]
            zed = dot(abreast(jnp.concatenate(sides, axis=1)), z_fwd[...])
            spec = dot(
                x_fwd[...], stacked(jnp.concatenate([zed[:, :256], zed[:, 256:]], axis=0))
            )
            real, imag = spec[:256], spec[256:]
            measured = jnp.concatenate(
                [inten[j, pl.ds(4 * h + k, 256, stride=8), :] for j in range(2)], axis=1
            )
            excess = 4.0 * (real * real + imag * imag - measured)
            residual = jnp.concatenate([excess * real, excess * imag], axis=0)
            back = dot(x_back[...], stacked(residual))
            out = dot(abreast(jnp.concatenate([back[:128], back[128:]], axis=1)), z_back[...])
            for c in range(2):
                for x in range(ROWS):
                    back_send[h, pl.ds(c * 16 + x * 4 + k, 32, stride=32), :] = out[
                        32 * x : 32 * (x + 1), 128 * c : 128 * (c + 1)
                    ]
            return carry

        lax.fori_loop(0, 4, row, 0)
        slab_sends(back_send, back_recv, slab_back_sem, h)

    for h in range(2):
        wait_arrived(back_recv, slab_back_sem, h)

    for pair in range(2):
        columns = [
            jnp.concatenate(
                [
                    back_recv[h, pl.ds((2 * pair + j) * 4 + k, 64, stride=16), :]
                    for h in range(2)
                    for k in range(4)
                ],
                axis=0,
            )
            for j in range(2)
        ]
        out = dot(y_back[...], stacked(jnp.concatenate(columns, axis=1)))
        for j in range(2):
            ydone[:, :, :, 2 * pair + j] = out[:, 128 * j : 128 * (j + 1)].reshape(4, 2, 2, 16, 128)
    done_copies = {}
    for t in (2, 1, 3):
        done_copies[t] = remote(
            ydone.at[lax.rem(yy + t, 4)], ydone_all.at[4 - t], peer_back_sem.at[t], "refl", peer_of(t)
        )
        done_copies[t].start()
    for t in (2, 1, 3):
        done_copies[t].wait_recv()

    def summed(b):
        totals = [jnp.zeros((ROWS, 16, 128), F32) for _ in range(4)]
        for t in range(4):
            if t == 0:
                real, imag = ydone[yy, 0, b], ydone[yy, 1, b]
            else:
                real, imag = ydone_all[t, 0, b], ydone_all[t, 1, b]
            cosine, sine = trig[t, 0, b], trig[t, 1, b]
            coef = mill[lax.rem(yy + t, 4)]
            across = imag * cosine - real * sine
            totals[0] = totals[0] + real * cosine + imag * sine
            for c in range(3):
                totals[1 + c] = totals[1 + c] + coef[c : c + 1][None] * across
        return totals

    for f, total in enumerate(summed(1)):
        part[f] = total
    part_copy = remote(part, part_recv, part_sem, "refl", mate_id)
    part_copy.start()
    totals = summed(0)

    came = ((has[1], up_y), (has[0], down_y), (has[3], up_x), (has[2], down_x))
    for (there, copy) in ((has[0], up_y), (has[1], down_y), (has[2], up_x), (has[3], down_x)):
        pl.when(there)(copy.wait_recv)
    sub = lax.broadcasted_iota(jnp.int32, (ROWS, 16, 128), 1)
    last = lax.broadcasted_iota(jnp.int32, (ROWS, 16, 128), 2)
    lapped = []
    for f in range(4):
        x = own[f]
        beside = jnp.concatenate([ex_recv[0, f][None], x[:3]], axis=0)
        beside = beside + jnp.concatenate([x[1:], ex_recv[1, f][None]], axis=0)
        low = ey_recv[0, 4 * f : 4 * f + 4, :][:, None, :]
        high = ey_recv[1, 4 * f : 4 * f + 4, :][:, None, :]
        beside = beside + jnp.where(sub == 0, low, pltpu.roll(x, 1, 1))
        beside = beside + jnp.where(sub == 15, high, pltpu.roll(x, 15, 1))
        beside = beside + jnp.where(last == 0, 0.0, pltpu.roll(x, 1, 2))
        beside = beside + jnp.where(last == 127, 0.0, pltpu.roll(x, 127, 2))
        lapped.append(6.0 * x - beside)

    part_copy.wait_recv()
    mask = sup[...].astype(F32)
    amp_out[...] = mask * (totals[0] + part_recv[0]) + 2.0 * EDGE_WEIGHT * mask * lapped[0]
    for c in range(3):
        disp_out[c] = (
            own[0] * (totals[1 + c] + part_recv[1 + c]) + 2.0 * STRAIN_WEIGHT * lapped[1 + c]
        )

    mate_copy.wait_send()
    for copy in mill_copies:
        copy.wait_send()
    for there, copy in zip(has, edges):
        pl.when(there)(copy.wait_send)
    for t in (1, 2, 3):
        obj_copies[t].wait_send()
        done_copies[t].wait_send()
    for h in range(2):
        wait_sent(fwd_send, fwd_recv, slab_sem, h)
        wait_sent(back_send, back_recv, slab_back_sem, h)
    part_copy.wait_send()


def body(amplitude, displacement, support, miller, shift_kz, intensity):
    vmem = pl.BlockSpec(memory_space=pltpu.VMEM)
    smem = pl.BlockSpec(memory_space=pltpu.SMEM)
    anywhere = pl.BlockSpec(memory_space=pl.ANY)
    block = (ROWS, 16, 128)
    sems = pltpu.SemaphoreType.DMA
    return pl.pallas_call(
        kernel,
        out_shape=(
            jax.ShapeDtypeStruct(block, F32),
            jax.ShapeDtypeStruct((3, *block), F32),
        ),
        in_specs=[vmem, vmem, anywhere, smem, smem, anywhere],
        out_specs=(vmem, vmem),
        scratch_shapes=[
            pltpu.VMEM(block, jnp.int32),
            pltpu.VMEM((2, 2048, 128), F32),
            pltpu.VMEM((4, *block), F32),
            pltpu.VMEM((4, *block), F32),
            pltpu.VMEM((4, 8, 128), F32),
            pltpu.VMEM((2, 16, 128), F32),
            pltpu.VMEM((2, 16, 128), F32),
            pltpu.VMEM((2, 4, 16, 128), F32),
            pltpu.VMEM((4, 2, 2, *block), F32),
            pltpu.VMEM((4, 2, 2, *block), F32),
            pltpu.VMEM((4, 2, 2, *block), F32),
            pltpu.VMEM((2, 768, 256), BF16),
            pltpu.VMEM((2, HALF, 128), F32),
            pltpu.VMEM((2, HALF, 128), F32),
            pltpu.VMEM((2, HALF, 128), F32),
            pltpu.VMEM((2, HALF, 128), F32),
            pltpu.VMEM((4, 2, 2, *block), F32),
            pltpu.VMEM((4, 2, 2, *block), F32),
            pltpu.VMEM((4, *block), F32),
            pltpu.VMEM((4, *block), F32),
            pltpu.VMEM((512, 768), BF16),
            pltpu.VMEM((256, 1536), BF16),
            pltpu.VMEM((512, 768), BF16),
            pltpu.VMEM((256, 1536), BF16),
            pltpu.VMEM((768, 512), BF16),
            pltpu.VMEM((1536, 256), BF16),
            sems((3,)),
            sems((2,)),
            sems((4, 2)),
            sems((4, 2)),
            sems((4, 2)),
            sems((4, 2)),
            sems((2, 2)),
            sems((2, 2)),
            sems((2,)),
        ],
        compiler_params=pltpu.CompilerParams(
            collective_id=0, has_side_effects=True, vmem_limit_bytes=56 * 1024 * 1024
        ),
        name="gradient",
    )(amplitude, displacement, support, miller, shift_kz, intensity.reshape(2048, 256))


def solution(mesh):
    placed = (
        P("slab", "refl", None),
        P(None, "slab", "refl", None),
        P("slab", None, None),
        P("refl", None),
        P("refl"),
        P("refl", None, "slab", None),
    )
    return jax.shard_map(
        body,
        mesh=mesh,
        in_specs=placed,
        out_specs=(P("slab", "refl", None), P(None, "slab", "refl", None)),
        check_vma=False,
    )
```

time: 190 us -> 100 us (0.53); the launches traced: 188 us -> 99.8 us
  Pallas kernels: 0 us -> 95.6 us
  blocking collectives: 74.6 us -> 0 us
  starting transfers between devices: 39.1 us -> 0 us
  matrix products: 30.1 us -> 0 us
  waiting for transfers between devices: 29.7 us -> 0 us
  other arithmetic: 8.34 us -> 0 us
    pallas_call x0 -> x1, Pallas kernels: none -> 95.6 us  [body(): pl.pallas_call(kernel, out_shape=(jax.ShapeDtypeStruct(block, F32), jax.S...]
    all_to_all x2 -> x0, blocking collectives: 74.6 us -> none  [the longest x1 43 us: body(): moved = lax.all_to_all(both, 'slab', 2, 1, tiled=True)]
    dot_general x24 -> x0, matrix products: 30.1 us -> none  [multiply(): jnp.einsum(pattern, operand, matrix, precision=lax.Precision.HIGH, prefer...]
    all_to_all x3 -> x0, starting transfers between devices: 28.9 us -> none  [the longest x2 25.2 us: everyone(): return lax.all_to_all(spread, axis, 0, 0, tiled=True)]
    all_to_all x3 -> x0, waiting for transfers between devices: 26.3 us -> none  [the longest x2 26.3 us: everyone(): return lax.all_to_all(spread, axis, 0, 0, tiled=True)]
    ppermute x4 -> x0, starting transfers between devices: 10.2 us -> none  [the longest x2 6.84 us: extended_2(): lax.ppermute(last, axis, up)]
    add x3 -> x0, other arithmetic: 4.03 us -> none  [the longest x1 1.99 us: body(): phase = miller_row[0] * d0 + miller_row[1] * d1 + miller_row[2] * d2 + turn]
    ppermute x4 -> x0, waiting for transfers between devices: 3.38 us -> none  [the longest x2 3.38 us: extended_2(): lax.ppermute(leading, axis, [(b, a) for a, b in up])]
  transfers between devices with their start and end apart: 7 -> 0, of which waited for: 3 -> 0; matrix products, arithmetic and copies ran while one was open for 1% -> 0% of each run, Pallas kernels for 0% -> 0%
where the time goes in v1:
time: 100 us; the launch traced here: 99.8 us
  Pallas kernels  95.6 us (96%)
  local copies, waits for them, and re-layouts  2.91 us (3%)
  between operations  1.29 us (1%)
    pallas_call x1, Pallas kernels, body(): pl.pallas_call(kernel, out_shape=(jax.ShapeDtypeStruct(block, F32), jax.S...  95.6 us
    unnamed x2, local copies, waits for them, and re-layouts  2.91 us

profile of v1, /device:TPU:1, one launch (start us, length us, event | category | flops | bytes accessed | tf_op | source)
XLA Modules:
  0.0 99.8 jit_solution(16956388045269463068)
XLA Ops:
  1.3 95.6 %gradient.1 = (f32[4,16,128]{2,1,0:T(8,128)}, f32[3,4,16,128]{3,2,1,0:T(8,128)}) custom-call(f32[4,16,128]{2,1,0:T(8,128)} %amp_ref.1, f32[3,4,16,128]{3,2,1,0:T(8,128)} %disp_ref.1, s32[4,128,128]{2,1,0:T(8,128)} %sup_hbm.1, s32[1,3]{1,0:T(1,128)} %miller_ref.1, s32[1]{0:T(128)S(6)} %copy.10.shift_ref, f32[2048,256]{1,0:T(8,128)} %bitcast.1), custom_call_target="tpu_custom_call" | custom-call | tf_op jit(solution)/shard_map/gradient/pallas_call | solution.py:427
  96.9 1.4 %copy.11 = f32[4,16,128]{2,1,0:T(8,128)} copy(f32[4,16,128]{2,1,0:T(8,128)} %get-tuple-element.4) | data formatting | bytes 65536
  98.3 1.5 %copy.12 = f32[3,4,16,128]{3,2,1,0:T(8,128)} copy(f32[3,4,16,128]{3,2,1,0:T(8,128)} %get-tuple-element.5) | data formatting | bytes 196608

commit v2 on v1

--- a/solution.py
+++ b/solution.py
@@ -14,7 +14,8 @@
 EDGE_WEIGHT = 0.05
 SLABS = 32
 ROWS = 4
-HALF = SLABS * 32
+WIDTH = 2
+LINES = SLABS * 16
 
 
 def sine_turns(v):
@@ -104,7 +105,7 @@
     amp_ref, disp_ref, sup_hbm, miller_ref, shift_ref, int_hbm,
     amp_out, disp_out,
     sup, inten, own, mate, mill, ey_send, ey_recv, ex_recv, trig, obj, obj_all, bcat,
-    fwd_send, fwd_recv, back_send, back_recv, ydone, ydone_all, part, part_recv,
+    fwd_send, fwd_recv, back_send, back_recv, ydone, ydone_all, part, part_own, part_recv, lapped,
     y_fwd, y_back, x_fwd, x_back, z_fwd, z_back,
     load_sem, mate_sem, mill_sem, edge_sem, peer_sem, peer_back_sem, slab_sem, slab_back_sem, part_sem,
 ):
@@ -178,12 +179,17 @@
             device_id_type=MESH,
         )
 
-    mate_copy = remote(own, mate, mate_sem, "refl", mate_id)
-    mate_copy.start()
+    def planes(p):
+        return pl.ds(WIDTH * p, WIDTH)
+
+    mate_copies = [
+        remote(own.at[:, planes(p)], mate.at[:, planes(p)], mate_sem.at[p], "refl", mate_id)
+        for p in range(2)
+    ]
     mill_copies = [
         remote(mill.at[yy], mill.at[yy], mill_sem.at[t], "refl", peer_of(t)) for t in (1, 2, 3)
     ]
-    for copy in mill_copies:
+    for copy in mill_copies + mate_copies:
         copy.start()
 
     has = (refl > 0, refl < 7, me > 0, me < SLABS - 1)
@@ -208,62 +214,45 @@
         return ((side & 1) * 4 + (i >> 6)) * 16 + (i & 15), (i >> 5) & 1
 
     fill_table(y_fwd, (512, 256), True, freq_y, place_y, True)
-    fill_table(y_back, (256, 512), False, freq_y, place_y, True)
-    fill_table(x_fwd, (512, 256), True, freq_plain, place_x, True)
-    fill_table(x_back, (256, 512), False, freq_plain, place_x, True)
-    fill_table(z_fwd, (256, 512), False, freq_plain, place_plain, False)
-    fill_table(z_back, (512, 256), True, freq_plain, place_plain, False)
-
-    for t in (1, 2, 3):
-        remote(mill.at[yy], mill.at[yy], mill_sem.at[t], "refl", peer_of(t)).wait_recv()
-    mate_copy.wait_recv()
+    for copy in mill_copies:
+        copy.wait_recv()
     lane = lax.broadcasted_iota(jnp.int32, (1, 1, 128), 2).astype(F32)
 
-    def objects(t, store):
+    def objects(t, p, ref):
         coef = mill[lax.rem(yy + t, 4)]
         m0, m1, m2, s = [coef[j : j + 1][None] for j in range(4)]
         turn = s * lane * (1.0 / 256.0)
         turn = turn - jnp.floor(turn)
         for b, fields in enumerate((own, mate)):
-            phase = m0 * fields[1] + m1 * fields[2] + m2 * fields[3]
+            weight, d0, d1, d2 = [fields[f, planes(p)] for f in range(4)]
+            phase = m0 * d0 + m1 * d1 + m2 * d2
             cosine, sine = cos_sin_turns(phase * (1.0 / (2 * math.pi)) + turn)
-            trig[t, 0, b] = cosine
-            trig[t, 1, b] = sine
-            weight = fields[0]
-            store(0, b, weight * cosine)
-            store(1, b, weight * sine)
-
-    def keep(t):
-        def store(c, b, value):
-            obj[t, c, b] = value
-        return store
-
-    def keep_own(c, b, value):
-        obj_all[yy, c, b] = value
-
-    obj_copies = {}
-    for t in (2, 1, 3):
-        objects(t, keep(t))
-        obj_copies[t] = remote(obj.at[t], obj_all.at[yy], peer_sem.at[t], "refl", peer_of(t))
-        obj_copies[t].start()
-    objects(0, keep_own)
-    for t in (2, 1, 3):
-        obj_copies[t].wait_recv()
-
-    for pair in range(2):
-        columns = [
-            obj_all[:, :, :, 2 * pair + j].reshape(256, 128) for j in range(2)
-        ]
-        bcat[pair] = stacked(jnp.concatenate(columns, axis=1))
-
-    def slab_sends(src, dst, sems, h):
+            trig[t, 0, b, planes(p)] = cosine
+            trig[t, 1, b, planes(p)] = sine
+            ref[0, b] = weight * cosine
+            ref[1, b] = weight * sine
+
+    obj_copies = [{}, {}]
+    for p in range(2):
+        mate_copies[p].wait_recv()
+        for t in (2, 1, 3):
+            objects(t, p, obj.at[t, p])
+            copy = remote(obj.at[t, p], obj_all.at[p, yy], peer_sem.at[p, t], "refl", peer_of(t))
+            copy.start()
+            obj_copies[p][t] = copy
+        objects(0, p, obj_all.at[p, yy])
+
+    def slab_sends(src, dst, sems, at, g):
+        def lines(i):
+            return (*at, pl.ds(pl.multiple_of(i * 16, 16), 16))
+
         def send(j, carry):
             to = lax.rem(me + j, SLABS)
             pltpu.make_async_remote_copy(
-                src_ref=src.at[h, pl.ds(pl.multiple_of(to * 32, 32), 32)],
-                dst_ref=dst.at[h, pl.ds(pl.multiple_of(me * 32, 32), 32)],
-                send_sem=sems.at[0, h],
-                recv_sem=sems.at[1, h],
+                src_ref=src.at[lines(to)],
+                dst_ref=dst.at[lines(me)],
+                send_sem=sems.at[0, g],
+                recv_sem=sems.at[1, g],
                 device_id={"slab": to},
                 device_id_type=MESH,
             ).start()
@@ -271,37 +260,53 @@
 
         lax.fori_loop(16, SLABS, send, 0)
         lax.fori_loop(1, 16, send, 0)
-        mine = pl.ds(pl.multiple_of(me * 32, 32), 32)
-        pltpu.make_async_copy(src.at[h, mine], dst.at[h, mine], sems.at[1, h]).start()
-
-    def wait_sent(src, dst, sems, h):
-        most = pl.ds(0, HALF - 32)
-        pltpu.make_async_copy(src.at[h, most], dst.at[h, most], sems.at[0, h]).wait()
-
-    def wait_arrived(dst, sems, h):
-        pltpu.make_async_copy(dst.at[h], dst.at[h], sems.at[1, h]).wait()
-
-    for h in range(2):
-        for pair in range(2):
-            out = dot(y_fwd[256 * h : 256 * (h + 1), :], bcat[pair])
+        pltpu.make_async_copy(src.at[lines(me)], dst.at[lines(me)], sems.at[1, g]).start()
+
+    def wait_sent(src, dst, sems, at, g):
+        most = (*at, pl.ds(0, LINES - 16))
+        pltpu.make_async_copy(src.at[most], dst.at[most], sems.at[0, g]).wait()
+
+    def wait_arrived(dst, sems, at, g):
+        pltpu.make_async_copy(dst.at[at], dst.at[at], sems.at[1, g]).wait()
+
+    whole = slice(None)
+    fwd_groups = ((0, whole), (1, 0), (1, 1))
+    back_groups = ((0, whole), (1, 0), (1, 1))
+
+    for p in range(2):
+        for t in (1, 3, 2):
+            obj_copies[p][t].wait_recv()
+        columns = [obj_all[p, :, :, :, j].reshape(256, 128) for j in range(WIDTH)]
+        bcat[...] = stacked(jnp.concatenate(columns, axis=1))
+        for h in range(2):
+            out = dot(y_fwd[256 * h : 256 * (h + 1), :], bcat[...])
             for k in range(4):
-                for j in range(2):
-                    fwd_send[h, pl.ds((2 * pair + j) * 4 + k, 64, stride=16), :] = out[
+                for j in range(WIDTH):
+                    fwd_send[p, h, pl.ds(4 * j + k, 64, stride=8), :] = out[
                         64 * k : 64 * (k + 1), 128 * j : 128 * (j + 1)
                     ]
-        slab_sends(fwd_send, fwd_recv, slab_sem, h)
-
+            if p == 1:
+                slab_sends(fwd_send, fwd_recv, slab_sem, fwd_groups[1 + h], 1 + h)
+        if p == 0:
+            slab_sends(fwd_send, fwd_recv, slab_sem, fwd_groups[0], 0)
+
+    fill_table(x_fwd, (512, 256), True, freq_plain, place_x, True)
+    fill_table(z_fwd, (256, 512), False, freq_plain, place_plain, False)
+    fill_table(x_back, (256, 512), False, freq_plain, place_x, True)
+    fill_table(z_back, (512, 256), True, freq_plain, place_plain, False)
+    fill_table(y_back, (256, 512), False, freq_y, place_y, True)
     for copy in int_copies:
         copy.wait()
 
     for h in range(2):
-        wait_arrived(fwd_recv, slab_sem, h)
+        for g in ((0, 1), (2,))[h]:
+            wait_arrived(fwd_recv, slab_sem, fwd_groups[g], g)
 
         def row(k, carry):
             sides = [
                 jnp.concatenate(
                     [
-                        fwd_recv[h, pl.ds(c * 16 + x * 4 + k, 32, stride=32), :]
+                        fwd_recv[x // 2, h, pl.ds(c * 8 + (x % 2) * 4 + k, 32, stride=16), :]
                         for x in range(ROWS)
                     ],
                     axis=0,
@@ -322,68 +327,19 @@
             out = dot(abreast(jnp.concatenate([back[:128], back[128:]], axis=1)), z_back[...])
             for c in range(2):
                 for x in range(ROWS):
-                    back_send[h, pl.ds(c * 16 + x * 4 + k, 32, stride=32), :] = out[
+                    back_send[h, x // 2, pl.ds(c * 8 + (x % 2) * 4 + k, 32, stride=16), :] = out[
                         32 * x : 32 * (x + 1), 128 * c : 128 * (c + 1)
                     ]
             return carry
 
         lax.fori_loop(0, 4, row, 0)
-        slab_sends(back_send, back_recv, slab_back_sem, h)
-
-    for h in range(2):
-        wait_arrived(back_recv, slab_back_sem, h)
-
-    for pair in range(2):
-        columns = [
-            jnp.concatenate(
-                [
-                    back_recv[h, pl.ds((2 * pair + j) * 4 + k, 64, stride=16), :]
-                    for h in range(2)
-                    for k in range(4)
-                ],
-                axis=0,
-            )
-            for j in range(2)
-        ]
-        out = dot(y_back[...], stacked(jnp.concatenate(columns, axis=1)))
-        for j in range(2):
-            ydone[:, :, :, 2 * pair + j] = out[:, 128 * j : 128 * (j + 1)].reshape(4, 2, 2, 16, 128)
-    done_copies = {}
-    for t in (2, 1, 3):
-        done_copies[t] = remote(
-            ydone.at[lax.rem(yy + t, 4)], ydone_all.at[4 - t], peer_back_sem.at[t], "refl", peer_of(t)
-        )
-        done_copies[t].start()
-    for t in (2, 1, 3):
-        done_copies[t].wait_recv()
-
-    def summed(b):
-        totals = [jnp.zeros((ROWS, 16, 128), F32) for _ in range(4)]
-        for t in range(4):
-            if t == 0:
-                real, imag = ydone[yy, 0, b], ydone[yy, 1, b]
-            else:
-                real, imag = ydone_all[t, 0, b], ydone_all[t, 1, b]
-            cosine, sine = trig[t, 0, b], trig[t, 1, b]
-            coef = mill[lax.rem(yy + t, 4)]
-            across = imag * cosine - real * sine
-            totals[0] = totals[0] + real * cosine + imag * sine
-            for c in range(3):
-                totals[1 + c] = totals[1 + c] + coef[c : c + 1][None] * across
-        return totals
-
-    for f, total in enumerate(summed(1)):
-        part[f] = total
-    part_copy = remote(part, part_recv, part_sem, "refl", mate_id)
-    part_copy.start()
-    totals = summed(0)
-
-    came = ((has[1], up_y), (has[0], down_y), (has[3], up_x), (has[2], down_x))
-    for (there, copy) in ((has[0], up_y), (has[1], down_y), (has[2], up_x), (has[3], down_x)):
+        for g in ((0,), (1, 2))[h]:
+            slab_sends(back_send, back_recv, slab_back_sem, back_groups[g], g)
+
+    for there, copy in ((has[0], up_y), (has[1], down_y), (has[2], up_x), (has[3], down_x)):
         pl.when(there)(copy.wait_recv)
     sub = lax.broadcasted_iota(jnp.int32, (ROWS, 16, 128), 1)
     last = lax.broadcasted_iota(jnp.int32, (ROWS, 16, 128), 2)
-    lapped = []
     for f in range(4):
         x = own[f]
         beside = jnp.concatenate([ex_recv[0, f][None], x[:3]], axis=0)
@@ -394,28 +350,85 @@
         beside = beside + jnp.where(sub == 15, high, pltpu.roll(x, 15, 1))
         beside = beside + jnp.where(last == 0, 0.0, pltpu.roll(x, 1, 2))
         beside = beside + jnp.where(last == 127, 0.0, pltpu.roll(x, 127, 2))
-        lapped.append(6.0 * x - beside)
-
-    part_copy.wait_recv()
-    mask = sup[...].astype(F32)
-    amp_out[...] = mask * (totals[0] + part_recv[0]) + 2.0 * EDGE_WEIGHT * mask * lapped[0]
-    for c in range(3):
-        disp_out[c] = (
-            own[0] * (totals[1 + c] + part_recv[1 + c]) + 2.0 * STRAIN_WEIGHT * lapped[1 + c]
-        )
-
-    mate_copy.wait_send()
-    for copy in mill_copies:
+        lapped[f] = 2.0 * (EDGE_WEIGHT if f == 0 else STRAIN_WEIGHT) * (6.0 * x - beside)
+
+    done_copies = [{}, {}]
+    for p in range(2):
+        for g in ((0, 1), (2,))[p]:
+            wait_arrived(back_recv, slab_back_sem, back_groups[g], g)
+        columns = [
+            jnp.concatenate(
+                [
+                    back_recv[h, p, pl.ds(4 * j + k, 64, stride=8), :]
+                    for h in range(2)
+                    for k in range(4)
+                ],
+                axis=0,
+            )
+            for j in range(WIDTH)
+        ]
+        out = dot(y_back[...], stacked(jnp.concatenate(columns, axis=1)))
+        for j in range(WIDTH):
+            ydone[p, :, :, :, j] = out[:, 128 * j : 128 * (j + 1)].reshape(4, 2, 2, 16, 128)
+        for t in (2, 1, 3):
+            copy = remote(
+                ydone.at[p, lax.rem(yy + t, 4)],
+                ydone_all.at[p, 4 - t],
+                peer_back_sem.at[p, t],
+                "refl",
+                peer_of(t),
+            )
+            copy.start()
+            done_copies[p][t] = copy
+
+    def summed(b, p):
+        totals = [jnp.zeros((WIDTH, 16, 128), F32) for _ in range(4)]
+        for t in range(4):
+            if t == 0:
+                real, imag = ydone[p, yy, 0, b], ydone[p, yy, 1, b]
+            else:
+                real, imag = ydone_all[p, t, 0, b], ydone_all[p, t, 1, b]
+            cosine, sine = trig[t, 0, b, planes(p)], trig[t, 1, b, planes(p)]
+            coef = mill[lax.rem(yy + t, 4)]
+            across = imag * cosine - real * sine
+            totals[0] = totals[0] + real * cosine + imag * sine
+            for c in range(3):
+                totals[1 + c] = totals[1 + c] + coef[c : c + 1][None] * across
+        return totals
+
+    part_copies = []
+    for p in range(2):
+        for t in (1, 3, 2):
+            done_copies[p][t].wait_recv()
+        for f, total in enumerate(summed(1, p)):
+            part[p, f] = total
+        copy = remote(part.at[p], part_recv.at[p], part_sem.at[p], "refl", mate_id)
+        copy.start()
+        part_copies.append(copy)
+        for f, total in enumerate(summed(0, p)):
+            part_own[p, f] = total
+
+    for p in range(2):
+        part_copies[p].wait_recv()
+        mask = sup[planes(p)].astype(F32)
+        amp_out[planes(p)] = mask * (part_own[p, 0] + part_recv[p, 0] + lapped[0, planes(p)])
+        for c in range(3):
+            disp_out[c, planes(p)] = (
+                own[0, planes(p)] * (part_own[p, 1 + c] + part_recv[p, 1 + c])
+                + lapped[1 + c, planes(p)]
+            )
+
+    for copy in mill_copies + mate_copies + part_copies:
         copy.wait_send()
     for there, copy in zip(has, edges):
         pl.when(there)(copy.wait_send)
-    for t in (1, 2, 3):
-        obj_copies[t].wait_send()
-        done_copies[t].wait_send()
-    for h in range(2):
-        wait_sent(fwd_send, fwd_recv, slab_sem, h)
-        wait_sent(back_send, back_recv, slab_back_sem, h)
-    part_copy.wait_send()
+    for p in range(2):
+        for t in (1, 2, 3):
+            obj_copies[p][t].wait_send()
+            done_copies[p][t].wait_send()
+    for g in range(3):
+        wait_sent(fwd_send, fwd_recv, slab_sem, fwd_groups[g], g)
+        wait_sent(back_send, back_recv, slab_back_sem, back_groups[g], g)
 
 
 def body(amplitude, displacement, support, miller, shift_kz, intensity):
@@ -423,6 +436,7 @@
     smem = pl.BlockSpec(memory_space=pltpu.SMEM)
     anywhere = pl.BlockSpec(memory_space=pl.ANY)
     block = (ROWS, 16, 128)
+    chunk = (WIDTH, 16, 128)
     sems = pltpu.SemaphoreType.DMA
     return pl.pallas_call(
         kernel,
@@ -442,16 +456,18 @@
             pltpu.VMEM((2, 16, 128), F32),
             pltpu.VMEM((2, 4, 16, 128), F32),
             pltpu.VMEM((4, 2, 2, *block), F32),
-            pltpu.VMEM((4, 2, 2, *block), F32),
-            pltpu.VMEM((4, 2, 2, *block), F32),
-            pltpu.VMEM((2, 768, 256), BF16),
-            pltpu.VMEM((2, HALF, 128), F32),
-            pltpu.VMEM((2, HALF, 128), F32),
-            pltpu.VMEM((2, HALF, 128), F32),
-            pltpu.VMEM((2, HALF, 128), F32),
-            pltpu.VMEM((4, 2, 2, *block), F32),
-            pltpu.VMEM((4, 2, 2, *block), F32),
-            pltpu.VMEM((4, *block), F32),
+            pltpu.VMEM((4, 2, 2, 2, *chunk), F32),
+            pltpu.VMEM((2, 4, 2, 2, *chunk), F32),
+            pltpu.VMEM((768, 256), BF16),
+            pltpu.VMEM((2, 2, LINES, 128), F32),
+            pltpu.VMEM((2, 2, LINES, 128), F32),
+            pltpu.VMEM((2, 2, LINES, 128), F32),
+            pltpu.VMEM((2, 2, LINES, 128), F32),
+            pltpu.VMEM((2, 4, 2, 2, *chunk), F32),
+            pltpu.VMEM((2, 4, 2, 2, *chunk), F32),
+            pltpu.VMEM((2, 4, *chunk), F32),
+            pltpu.VMEM((2, 4, *chunk), F32),
+            pltpu.VMEM((2, 4, *chunk), F32),
             pltpu.VMEM((4, *block), F32),
             pltpu.VMEM((512, 768), BF16),
             pltpu.VMEM((256, 1536), BF16),
@@ -460,14 +476,14 @@
             pltpu.VMEM((768, 512), BF16),
             pltpu.VMEM((1536, 256), BF16),
             sems((3,)),
-            sems((2,)),
+            sems((2, 2)),
             sems((4, 2)),
             sems((4, 2)),
-            sems((4, 2)),
-            sems((4, 2)),
+            sems((2, 4, 2)),
+            sems((2, 4, 2)),
+            sems((2, 3)),
+            sems((2, 3)),
             sems((2, 2)),
-            sems((2, 2)),
-            sems((2,)),
         ],
         compiler_params=pltpu.CompilerParams(
             collective_id=0, has_side_effects=True, vmem_limit_bytes=56 * 1024 * 1024

time: 100 us -> 93.6 us (0.936)
  Pallas kernels: 95.6 us -> 89 us
    pallas_call x1, Pallas kernels: 95.6 us -> 89 us  [body(): pl.pallas_call(kernel, out_shape=(jax.ShapeDtypeStruct(block, F32), jax.S...]
where the time goes in v2:
time: 93.6 us; the launch traced here: 93.2 us
  Pallas kernels  89 us (95%)
  local copies, waits for them, and re-layouts  2.91 us (3%)
  between operations  1.29 us (1%)
    pallas_call x1, Pallas kernels, body(): pl.pallas_call(kernel, out_shape=(jax.ShapeDtypeStruct(block, F32), jax.S...  89 us
    unnamed x2, local copies, waits for them, and re-layouts  2.91 us

profile of v2, /device:TPU:1, one launch (start us, length us, event | category | flops | bytes accessed | tf_op | source)
XLA Modules:
  0.0 93.2 jit_solution(10031519165336741395)
XLA Ops:
  1.3 89.0 %gradient.1 = (f32[4,16,128]{2,1,0:T(8,128)}, f32[3,4,16,128]{3,2,1,0:T(8,128)}) custom-call(f32[4,16,128]{2,1,0:T(8,128)} %amp_ref.1, f32[3,4,16,128]{3,2,1,0:T(8,128)} %disp_ref.1, s32[4,128,128]{2,1,0:T(8,128)} %sup_hbm.1, s32[1,3]{1,0:T(1,128)} %miller_ref.1, s32[1]{0:T(128)S(6)} %copy.10.shift_ref, f32[2048,256]{1,0:T(8,128)} %bitcast.1), custom_call_target="tpu_custom_call" | custom-call | tf_op jit(solution)/shard_map/gradient/pallas_call | solution.py:441
  90.2 1.4 %copy.11 = f32[4,16,128]{2,1,0:T(8,128)} copy(f32[4,16,128]{2,1,0:T(8,128)} %get-tuple-element.4) | data formatting | bytes 65536
  91.6 1.5 %copy.12 = f32[3,4,16,128]{3,2,1,0:T(8,128)} copy(f32[3,4,16,128]{3,2,1,0:T(8,128)} %get-tuple-element.5) | data formatting | bytes 196608

commit v3 on v2

--- a/solution.py
+++ b/solution.py
@@ -210,37 +210,40 @@
         pl.when(jnp.logical_not(there))(nothing(ref, at))
 
     def place_y(i):
-        side = ((i >> 4) & 1) + zh
-        return ((side & 1) * 4 + (i >> 6)) * 16 + (i & 15), (i >> 5) & 1
+        side = ((i >> 5) & 1) + zh
+        return ((side & 1) * 4 + (i >> 6)) * 16 + (i & 15), (i >> 4) & 1
 
     fill_table(y_fwd, (512, 256), True, freq_y, place_y, True)
     for copy in mill_copies:
         copy.wait_recv()
     lane = lax.broadcasted_iota(jnp.int32, (1, 1, 128), 2).astype(F32)
 
-    def objects(t, p, ref):
+    def objects(t, p, b, ref):
         coef = mill[lax.rem(yy + t, 4)]
         m0, m1, m2, s = [coef[j : j + 1][None] for j in range(4)]
         turn = s * lane * (1.0 / 256.0)
         turn = turn - jnp.floor(turn)
-        for b, fields in enumerate((own, mate)):
-            weight, d0, d1, d2 = [fields[f, planes(p)] for f in range(4)]
-            phase = m0 * d0 + m1 * d1 + m2 * d2
-            cosine, sine = cos_sin_turns(phase * (1.0 / (2 * math.pi)) + turn)
-            trig[t, 0, b, planes(p)] = cosine
-            trig[t, 1, b, planes(p)] = sine
-            ref[0, b] = weight * cosine
-            ref[1, b] = weight * sine
-
-    obj_copies = [{}, {}]
-    for p in range(2):
-        mate_copies[p].wait_recv()
-        for t in (2, 1, 3):
-            objects(t, p, obj.at[t, p])
-            copy = remote(obj.at[t, p], obj_all.at[p, yy], peer_sem.at[p, t], "refl", peer_of(t))
-            copy.start()
-            obj_copies[p][t] = copy
-        objects(0, p, obj_all.at[p, yy])
+        weight, d0, d1, d2 = [(own, mate)[b][f, planes(p)] for f in range(4)]
+        phase = m0 * d0 + m1 * d1 + m2 * d2
+        cosine, sine = cos_sin_turns(phase * (1.0 / (2 * math.pi)) + turn)
+        trig[t, 0, b, planes(p)] = cosine
+        trig[t, 1, b, planes(p)] = sine
+        ref[0] = weight * cosine
+        ref[1] = weight * sine
+
+    obj_copies = {}
+    for b in range(2):
+        for p in range(2):
+            if b == 1:
+                mate_copies[p].wait_recv()
+            for t in (2, 1, 3):
+                objects(t, p, b, obj.at[t, p, b])
+                copy = remote(
+                    obj.at[t, p, b], obj_all.at[p, yy, b], peer_sem.at[p, b, t], "refl", peer_of(t)
+                )
+                copy.start()
+                obj_copies[p, b, t] = copy
+            objects(0, p, b, obj_all.at[p, yy, b])
 
     def slab_sends(src, dst, sems, at, g):
         def lines(i):
@@ -270,25 +273,28 @@
         pltpu.make_async_copy(dst.at[at], dst.at[at], sems.at[1, g]).wait()
 
     whole = slice(None)
-    fwd_groups = ((0, whole), (1, 0), (1, 1))
+    fwd_groups = ((0, 0), (0, 1), (1, whole))
     back_groups = ((0, whole), (1, 0), (1, 1))
 
+    def why(h, p):
+        out = dot(y_fwd[256 * h : 256 * (h + 1), :], bcat[p])
+        for k in range(4):
+            for j in range(WIDTH):
+                fwd_send[h, p, pl.ds(4 * j + k, 64, stride=8), :] = out[
+                    64 * k : 64 * (k + 1), 128 * j : 128 * (j + 1)
+                ]
+
     for p in range(2):
-        for t in (1, 3, 2):
-            obj_copies[p][t].wait_recv()
+        for b in range(2):
+            for t in (1, 3, 2):
+                obj_copies[p, b, t].wait_recv()
         columns = [obj_all[p, :, :, :, j].reshape(256, 128) for j in range(WIDTH)]
-        bcat[...] = stacked(jnp.concatenate(columns, axis=1))
-        for h in range(2):
-            out = dot(y_fwd[256 * h : 256 * (h + 1), :], bcat[...])
-            for k in range(4):
-                for j in range(WIDTH):
-                    fwd_send[p, h, pl.ds(4 * j + k, 64, stride=8), :] = out[
-                        64 * k : 64 * (k + 1), 128 * j : 128 * (j + 1)
-                    ]
-            if p == 1:
-                slab_sends(fwd_send, fwd_recv, slab_sem, fwd_groups[1 + h], 1 + h)
-        if p == 0:
-            slab_sends(fwd_send, fwd_recv, slab_sem, fwd_groups[0], 0)
+        bcat[p] = stacked(jnp.concatenate(columns, axis=1))
+        why(0, p)
+        slab_sends(fwd_send, fwd_recv, slab_sem, fwd_groups[p], p)
+    for p in range(2):
+        why(1, p)
+    slab_sends(fwd_send, fwd_recv, slab_sem, fwd_groups[2], 2)
 
     fill_table(x_fwd, (512, 256), True, freq_plain, place_x, True)
     fill_table(z_fwd, (256, 512), False, freq_plain, place_plain, False)
@@ -306,7 +312,7 @@
             sides = [
                 jnp.concatenate(
                     [
-                        fwd_recv[x // 2, h, pl.ds(c * 8 + (x % 2) * 4 + k, 32, stride=16), :]
+                        fwd_recv[h, x // 2, pl.ds(c * 8 + (x % 2) * 4 + k, 32, stride=16), :]
                         for x in range(ROWS)
                     ],
                     axis=0,
@@ -352,7 +358,7 @@
         beside = beside + jnp.where(last == 127, 0.0, pltpu.roll(x, 127, 2))
         lapped[f] = 2.0 * (EDGE_WEIGHT if f == 0 else STRAIN_WEIGHT) * (6.0 * x - beside)
 
-    done_copies = [{}, {}]
+    done_copies = {}
     for p in range(2):
         for g in ((0, 1), (2,))[p]:
             wait_arrived(back_recv, slab_back_sem, back_groups[g], g)
@@ -370,24 +376,27 @@
         out = dot(y_back[...], stacked(jnp.concatenate(columns, axis=1)))
         for j in range(WIDTH):
             ydone[p, :, :, :, j] = out[:, 128 * j : 128 * (j + 1)].reshape(4, 2, 2, 16, 128)
-        for t in (2, 1, 3):
-            copy = remote(
-                ydone.at[p, lax.rem(yy + t, 4)],
-                ydone_all.at[p, 4 - t],
-                peer_back_sem.at[p, t],
-                "refl",
-                peer_of(t),
-            )
-            copy.start()
-            done_copies[p][t] = copy
+        for b in (1, 0):
+            for t in (2, 1, 3):
+                copy = remote(
+                    ydone.at[p, lax.rem(yy + t, 4), b],
+                    ydone_all.at[p, 4 - t, b],
+                    peer_back_sem.at[p, b, t],
+                    "refl",
+                    peer_of(t),
+                )
+                copy.start()
+                done_copies[p, b, t] = copy
 
     def summed(b, p):
+        for t in (1, 3, 2):
+            done_copies[p, b, t].wait_recv()
         totals = [jnp.zeros((WIDTH, 16, 128), F32) for _ in range(4)]
         for t in range(4):
             if t == 0:
-                real, imag = ydone[p, yy, 0, b], ydone[p, yy, 1, b]
+                real, imag = ydone[p, yy, b, 0], ydone[p, yy, b, 1]
             else:
-                real, imag = ydone_all[p, t, 0, b], ydone_all[p, t, 1, b]
+                real, imag = ydone_all[p, t, b, 0], ydone_all[p, t, b, 1]
             cosine, sine = trig[t, 0, b, planes(p)], trig[t, 1, b, planes(p)]
             coef = mill[lax.rem(yy + t, 4)]
             across = imag * cosine - real * sine
@@ -398,13 +407,12 @@
 
     part_copies = []
     for p in range(2):
-        for t in (1, 3, 2):
-            done_copies[p][t].wait_recv()
         for f, total in enumerate(summed(1, p)):
             part[p, f] = total
         copy = remote(part.at[p], part_recv.at[p], part_sem.at[p], "refl", mate_id)
         copy.start()
         part_copies.append(copy)
+    for p in range(2):
         for f, total in enumerate(summed(0, p)):
             part_own[p, f] = total
 
@@ -422,10 +430,9 @@
         copy.wait_send()
     for there, copy in zip(has, edges):
         pl.when(there)(copy.wait_send)
-    for p in range(2):
-        for t in (1, 2, 3):
-            obj_copies[p][t].wait_send()
-            done_copies[p][t].wait_send()
+    for at in obj_copies:
+        obj_copies[at].wait_send()
+        done_copies[at].wait_send()
     for g in range(3):
         wait_sent(fwd_send, fwd_recv, slab_sem, fwd_groups[g], g)
         wait_sent(back_send, back_recv, slab_back_sem, back_groups[g], g)
@@ -458,7 +465,7 @@
             pltpu.VMEM((4, 2, 2, *block), F32),
             pltpu.VMEM((4, 2, 2, 2, *chunk), F32),
             pltpu.VMEM((2, 4, 2, 2, *chunk), F32),
-            pltpu.VMEM((768, 256), BF16),
+            pltpu.VMEM((2, 768, 256), BF16),
             pltpu.VMEM((2, 2, LINES, 128), F32),
             pltpu.VMEM((2, 2, LINES, 128), F32),
             pltpu.VMEM((2, 2, LINES, 128), F32),
@@ -479,8 +486,8 @@
             sems((2, 2)),
             sems((4, 2)),
             sems((4, 2)),
-            sems((2, 4, 2)),
-            sems((2, 4, 2)),
+            sems((2, 2, 4, 2)),
+            sems((2, 2, 4, 2)),
             sems((2, 3)),
             sems((2, 3)),
             sems((2, 2)),

time: 93.6 us -> 89.3 us (0.954)
  Pallas kernels: 89 us -> 84.8 us
    pallas_call x1, Pallas kernels: 89 us -> 84.8 us  [body(): pl.pallas_call(kernel, out_shape=(jax.ShapeDtypeStruct(block, F32), jax.S...]
where the time goes in v3:
time: 89.3 us; the launch traced here: 89 us
  Pallas kernels  84.8 us (95%)
  local copies, waits for them, and re-layouts  2.91 us (3%)
  between operations  1.29 us (1%)
    pallas_call x1, Pallas kernels, body(): pl.pallas_call(kernel, out_shape=(jax.ShapeDtypeStruct(block, F32), jax.S...  84.8 us
    unnamed x2, local copies, waits for them, and re-layouts  2.91 us

profile of v3, /device:TPU:1, one launch (start us, length us, event | category | flops | bytes accessed | tf_op | source)
XLA Modules:
  0.0 89.0 jit_solution(4069102890426367242)
XLA Ops:
  1.3 84.8 %gradient.1 = (f32[4,16,128]{2,1,0:T(8,128)}, f32[3,4,16,128]{3,2,1,0:T(8,128)}) custom-call(f32[4,16,128]{2,1,0:T(8,128)} %amp_ref.1, f32[3,4,16,128]{3,2,1,0:T(8,128)} %disp_ref.1, s32[4,128,128]{2,1,0:T(8,128)} %sup_hbm.1, s32[1,3]{1,0:T(1,128)} %miller_ref.1, s32[1]{0:T(128)S(6)} %copy.10.shift_ref, f32[2048,256]{1,0:T(8,128)} %bitcast.1), custom_call_target="tpu_custom_call" | custom-call | tf_op jit(solution)/shard_map/gradient/pallas_call | solution.py:448
  86.1 1.4 %copy.11 = f32[4,16,128]{2,1,0:T(8,128)} copy(f32[4,16,128]{2,1,0:T(8,128)} %get-tuple-element.4) | data formatting | bytes 65536
  87.5 1.5 %copy.12 = f32[3,4,16,128]{3,2,1,0:T(8,128)} copy(f32[3,4,16,128]{3,2,1,0:T(8,128)} %get-tuple-element.5) | data formatting | bytes 196608

commit v4 on v3

v4 whole, which is shorter than its diff:
```python
import math

import jax
import jax.numpy as jnp
from jax import lax
from jax.experimental import pallas as pl
from jax.experimental.pallas import tpu as pltpu
from jax.sharding import PartitionSpec as P

MESH = pl.DeviceIdType.MESH
F32 = jnp.float32
BF16 = jnp.bfloat16
STRAIN_WEIGHT = 0.05
EDGE_WEIGHT = 0.05
SLABS = 32
ROWS = 4
WIDTH = 2
TEAM = SLABS // 2
LINES = TEAM * 16
BLOCKS = ((0, 1), (1, 1), (1, 0))


def sine_turns(v):
    w = v * v
    total = jnp.full_like(v, -((2 * math.pi) ** 11) / math.factorial(11))
    for power in (9, 7, 5, 3, 1):
        sign = 1.0 if power % 4 == 1 else -1.0
        total = total * w + sign * (2 * math.pi) ** power / math.factorial(power)
    return total * v


def cos_sin_turns(t):
    t = t - jnp.floor(t + 0.5)
    size = jnp.abs(t)
    cosine = sine_turns(0.25 - size)
    sine = sine_turns(0.25 - jnp.abs(size - 0.25))
    return cosine, jnp.where(t < 0.0, -sine, sine)


def split(x):
    high = x.astype(BF16)
    low = (x - high.astype(F32)).astype(BF16)
    return high, low


def stacked(x):
    high, low = split(x)
    return jnp.concatenate([high, low, high], axis=0)


def abreast(x):
    high, low = split(x)
    return jnp.concatenate([high, low, high], axis=1)


def dot(a, b):
    return jnp.dot(a, b, preferred_element_type=F32)


def freq_plain(i):
    return i & 255, i >> 8


def place_plain(i):
    return i & 127, i >> 7


def fill_table(ref, shape, row_is_freq, freq, place, on_left):
    rows, cols = shape
    chunk = 32

    def step(j, carry):
        start = pl.multiple_of(j * chunk, chunk)
        row = lax.broadcasted_iota(jnp.int32, (chunk, cols), 0) + start
        col = lax.broadcasted_iota(jnp.int32, (chunk, cols), 1)
        if row_is_freq:
            k, kc = freq(row)
            n, nc = place(col)
        else:
            k, kc = freq(col)
            n, nc = place(row)
        turns = ((k * n + 64 * (kc - nc) + 128) & 255) - 128
        t = turns.astype(F32) * (1.0 / 256.0)
        high, low = split(sine_turns(0.25 - jnp.abs(t)) * (1.0 / 16.0))
        if on_left:
            ref[pl.ds(start, chunk), 0:cols] = high
            ref[pl.ds(start, chunk), cols : 2 * cols] = high
            ref[pl.ds(start, chunk), 2 * cols : 3 * cols] = low
        else:
            ref[pl.ds(start, chunk), :] = high
            ref[pl.ds(pl.multiple_of(rows + start, chunk), chunk), :] = high
            ref[pl.ds(pl.multiple_of(2 * rows + start, chunk), chunk), :] = low
        return carry

    lax.fori_loop(0, rows // chunk, step, 0)


def kernel(
    amp_ref, disp_ref, sup_hbm, miller_ref, shift_ref, int_hbm,
    amp_out, disp_out,
    sup, inten, raw, mill, ey_send, ey_recv, ex_recv, trig, obj, obj_all, bcat,
    fwd_send, fwd_recv, back_send, back_recv, ydone, ydone_all, part, part_recv, lapped,
    y_fwd, y_back, x_fwd, x_back, z_fwd, z_back,
    load_sem, raw_sem, mill_sem, edge_sem, peer_sem, peer_back_sem, slab_sem, slab_back_sem, part_sem,
):
    refl = lax.axis_index("refl")
    me = lax.axis_index("slab")
    zh = refl // 4
    yy = lax.rem(refl, 4)
    team = me // TEAM
    own = raw.at[0, 0]

    def peer_of(t):
        return {"refl": zh * 4 + lax.rem(yy + t, 4)}

    def across(b, q):
        return {"refl": lax.rem(refl + 4 * b, 8), "slab": lax.rem(me + TEAM * q, SLABS)}

    sup_copy = pltpu.make_async_copy(
        sup_hbm.at[:, pl.ds(pl.multiple_of(refl * 16, 16), 16), :], sup, load_sem.at[0]
    )
    sup_copy.start()
    int_copies = [
        pltpu.make_async_copy(int_hbm.at[:, pl.ds(128 * j, 128)], inten.at[j], load_sem.at[1 + j])
        for j in range(2)
    ]
    for copy in int_copies:
        copy.start()

    barrier = pltpu.get_barrier_semaphore()

    def greet_slab(j, carry):
        pl.semaphore_signal(
            barrier, inc=1, device_id={"slab": lax.rem(me + j, SLABS)}, device_id_type=MESH
        )
        return carry

    def greet_refl(j, carry):
        pl.semaphore_signal(
            barrier, inc=1, device_id={"refl": lax.rem(refl + j, 8)}, device_id_type=MESH
        )
        return carry

    lax.fori_loop(1, 8, greet_refl, 0)
    lax.fori_loop(1, SLABS, greet_slab, 0)
    pl.semaphore_signal(barrier, inc=1, device_id=across(1, 1), device_id_type=MESH)

    own[1:4] = disp_ref[...]
    lane_row = lax.broadcasted_iota(jnp.int32, (8, 128), 0)
    tile = jnp.where(
        lane_row == 0,
        miller_ref[0, 0].astype(F32),
        jnp.where(
            lane_row == 1,
            miller_ref[0, 1].astype(F32),
            jnp.where(lane_row == 2, miller_ref[0, 2].astype(F32), shift_ref[0].astype(F32)),
        ),
    )
    mill[yy] = tile
    sup_copy.wait()
    mask = sup[...].astype(F32)
    own[0] = mask * amp_ref[...]
    for f in range(4):
        for x in range(ROWS):
            at = f * 4 + x
            ey_send[0, at : at + 1, :] = own[f, x, 0:1, :]
            ey_send[1, at : at + 1, :] = own[f, x, 15:16, :]

    pl.semaphore_wait(barrier, 39)

    def remote(src, dst, sems, target):
        return pltpu.make_async_remote_copy(
            src_ref=src,
            dst_ref=dst,
            send_sem=sems.at[0],
            recv_sem=sems.at[1],
            device_id=target,
            device_id_type=MESH,
        )

    def planes(p):
        return pl.ds(WIDTH * p, WIDTH)

    raw_copies = {
        (b, q, p): remote(
            raw.at[0, 0, :, planes(p)], raw.at[b, q, :, planes(p)], raw_sem.at[b, q, p], across(b, q)
        )
        for p in range(2)
        for b, q in BLOCKS
    }
    mill_copies = [
        remote(mill.at[yy], mill.at[yy], mill_sem.at[t], peer_of(t)) for t in (1, 2, 3)
    ]
    for copy in mill_copies + list(raw_copies.values()):
        copy.start()

    has = (refl > 0, refl < 7, me > 0, me < SLABS - 1)
    down_y = remote(ey_send.at[0], ey_recv.at[1], edge_sem.at[0], {"refl": lax.rem(refl + 7, 8)})
    up_y = remote(ey_send.at[1], ey_recv.at[0], edge_sem.at[1], {"refl": lax.rem(refl + 1, 8)})
    down_x = remote(own.at[:, 0], ex_recv.at[1], edge_sem.at[2], {"slab": lax.rem(me + SLABS - 1, SLABS)})
    up_x = remote(own.at[:, 3], ex_recv.at[0], edge_sem.at[3], {"slab": lax.rem(me + 1, SLABS)})
    edges = (down_y, up_y, down_x, up_x)
    for there, copy in zip(has, edges):
        pl.when(there)(copy.start)

    def nothing(ref, at):
        def fill():
            ref[at] = jnp.zeros(ref.shape[1:], F32)
        return fill

    for there, ref, at in zip(has, (ey_recv, ey_recv, ex_recv, ex_recv), (0, 1, 0, 1)):
        pl.when(jnp.logical_not(there))(nothing(ref, at))

    def place_y(i):
        side = ((i >> 5) & 1) + zh
        return ((side & 1) * 4 + (i >> 6)) * 16 + (i & 15), (i >> 4) & 1

    def freq_y(i):
        return 8 * (TEAM * team + ((i >> 1) & 15)) + 4 * (i >> 7) + ((i >> 5) & 3), i & 1

    def place_x(i):
        side = ((i >> 6) & 1) + team
        return 64 * (side & 1) + 4 * (i & 15) + 2 * ((i >> 5) & 1) + ((i >> 4) & 1), i >> 7

    fill_table(y_fwd, (256, 256), True, freq_y, place_y, True)
    for copy in mill_copies:
        copy.wait_recv()
    lane = lax.broadcasted_iota(jnp.int32, (1, 1, 128), 2).astype(F32)

    def objects(t, p, b, q, ref):
        coef = mill[lax.rem(yy + t, 4)]
        m0, m1, m2, s = [coef[j : j + 1][None] for j in range(4)]
        turn = s * lane * (1.0 / 256.0)
        turn = turn - jnp.floor(turn)
        weight, d0, d1, d2 = [raw[b, q, f, planes(p)] for f in range(4)]
        phase = m0 * d0 + m1 * d1 + m2 * d2
        cosine, sine = cos_sin_turns(phase * (1.0 / (2 * math.pi)) + turn)
        trig[t, 0, b, q, planes(p)] = cosine
        trig[t, 1, b, q, planes(p)] = sine
        ref[0] = weight * cosine
        ref[1] = weight * sine

    obj_copies = {}

    def object_block(p, b, q):
        for t in (2, 1, 3):
            objects(t, p, b, q, obj.at[t, p, q, b])
            copy = remote(
                obj.at[t, p, q, b], obj_all.at[p, q, yy, b], peer_sem.at[p, q, b, t], peer_of(t)
            )
            copy.start()
            obj_copies[p, q, b, t] = copy
        objects(0, p, b, q, obj_all.at[p, q, yy, b])

    for p in range(2):
        object_block(p, 0, 0)
    for p in range(2):
        for b, q in BLOCKS:
            raw_copies[b, q, p].wait_recv()
            object_block(p, b, q)

    def slab_sends(src, dst, sems, h, p):
        def lines(i):
            return (h, p, slice(None), pl.ds(pl.multiple_of(lax.rem(i, TEAM) * 16, 16), 16))

        def send(j, carry):
            to = TEAM * team + lax.rem(me + j, TEAM)
            pltpu.make_async_remote_copy(
                src_ref=src.at[lines(to)],
                dst_ref=dst.at[lines(me)],
                send_sem=sems.at[0, h, p],
                recv_sem=sems.at[1, h, p],
                device_id={"slab": to},
                device_id_type=MESH,
            ).start()
            return carry

        lax.fori_loop(1, TEAM, send, 0)
        pltpu.make_async_copy(src.at[lines(me)], dst.at[lines(me)], sems.at[1, h, p]).start()

    def wait_sent(src, dst, sems, h, p):
        most = (h, p, slice(None), pl.ds(0, LINES - 16))
        pltpu.make_async_copy(src.at[most], dst.at[most], sems.at[0, h, p]).wait()

    def wait_arrived(dst, sems, h, p):
        pltpu.make_async_copy(dst.at[h, p], dst.at[h, p], sems.at[1, h, p]).wait()

    for p in range(2):
        for b, q in ((0, 0), *BLOCKS):
            for t in (1, 3, 2):
                obj_copies[p, q, b, t].wait_recv()
        for q in range(2):
            columns = [obj_all[p, q, :, :, :, j].reshape(256, 128) for j in range(WIDTH)]
            bcat[q] = stacked(jnp.concatenate(columns, axis=1))
        for h in range(2):
            for q in range(2):
                out = dot(y_fwd[128 * h : 128 * (h + 1), :], bcat[q])
                for k in range(4):
                    for j in range(WIDTH):
                        fwd_send[h, p, q, pl.ds(4 * j + k, 32, stride=8), :] = out[
                            32 * k : 32 * (k + 1), 128 * j : 128 * (j + 1)
                        ]
            slab_sends(fwd_send, fwd_recv, slab_sem, h, p)

    fill_table(x_fwd, (512, 256), True, freq_plain, place_x, True)
    fill_table(z_fwd, (256, 512), False, freq_plain, place_plain, False)
    fill_table(x_back, (256, 512), False, freq_plain, place_x, True)
    fill_table(z_back, (512, 256), True, freq_plain, place_plain, False)
    fill_table(y_back, (256, 256), False, freq_y, place_y, True)
    for copy in int_copies:
        copy.wait()

    for h in range(2):
        for p in range(2):
            wait_arrived(fwd_recv, slab_sem, h, p)

        def row(k, carry):
            sides = [
                jnp.concatenate(
                    [
                        fwd_recv[h, p, q, pl.ds(c * 8 + 4 * j + k, 16, stride=16), :]
                        for q in range(2)
                        for p in range(2)
                        for j in range(WIDTH)
                    ],
                    axis=0,
                )
                for c in range(2)
            ]
            zed = dot(abreast(jnp.concatenate(sides, axis=1)), z_fwd[...])
            spec = dot(
                x_fwd[...], stacked(jnp.concatenate([zed[:, :256], zed[:, 256:]], axis=0))
            )
            real, imag = spec[:256], spec[256:]
            measured = jnp.concatenate(
                [inten[j, pl.ds(4 * h + k, 256, stride=8), :] for j in range(2)], axis=1
            )
            excess = 4.0 * (real * real + imag * imag - measured)
            residual = jnp.concatenate([excess * real, excess * imag], axis=0)
            back = dot(x_back[...], stacked(residual))
            out = dot(abreast(jnp.concatenate([back[:128], back[128:]], axis=1)), z_back[...])
            for c in range(2):
                for at in range(8):
                    q, p, j = at // 4, at // 2 % 2, at % 2
                    back_send[h, p, q, pl.ds(c * 8 + 4 * j + k, 16, stride=16), :] = out[
                        16 * at : 16 * (at + 1), 128 * c : 128 * (c + 1)
                    ]
            return carry

        lax.fori_loop(0, 4, row, 0)
        for p in range(2):
            slab_sends(back_send, back_recv, slab_back_sem, h, p)

    for there, copy in ((has[0], up_y), (has[1], down_y), (has[2], up_x), (has[3], down_x)):
        pl.when(there)(copy.wait_recv)
    sub = lax.broadcasted_iota(jnp.int32, (ROWS, 16, 128), 1)
    last = lax.broadcasted_iota(jnp.int32, (ROWS, 16, 128), 2)
    for f in range(4):
        x = own[f]
        beside = jnp.concatenate([ex_recv[0, f][None], x[:3]], axis=0)
        beside = beside + jnp.concatenate([x[1:], ex_recv[1, f][None]], axis=0)
        low = ey_recv[0, 4 * f : 4 * f + 4, :][:, None, :]
        high = ey_recv[1, 4 * f : 4 * f + 4, :][:, None, :]
        beside = beside + jnp.where(sub == 0, low, pltpu.roll(x, 1, 1))
        beside = beside + jnp.where(sub == 15, high, pltpu.roll(x, 15, 1))
        beside = beside + jnp.where(last == 0, 0.0, pltpu.roll(x, 1, 2))
        beside = beside + jnp.where(last == 127, 0.0, pltpu.roll(x, 127, 2))
        lapped[f] = 2.0 * (EDGE_WEIGHT if f == 0 else STRAIN_WEIGHT) * (6.0 * x - beside)

    done_copies = {}
    for p in range(2):
        for h in range(2):
            wait_arrived(back_recv, slab_back_sem, h, p)
        for q in range(2):
            columns = [
                jnp.concatenate(
                    [
                        back_recv[h, p, q, pl.ds(4 * j + k, 32, stride=8), :]
                        for h in range(2)
                        for k in range(4)
                    ],
                    axis=0,
                )
                for j in range(WIDTH)
            ]
            out = dot(y_back[...], stacked(jnp.concatenate(columns, axis=1)))
            for j in range(WIDTH):
                ydone[p, q, :, :, :, j] = out[:, 128 * j : 128 * (j + 1)].reshape(4, 2, 2, 16, 128)
        for b, q in ((1, 0), (1, 1), (0, 1), (0, 0)):
            for t in (2, 1, 3):
                copy = remote(
                    ydone.at[p, q, lax.rem(yy + t, 4), b],
                    ydone_all.at[p, q, 4 - t, b],
                    peer_back_sem.at[p, q, b, t],
                    peer_of(t),
                )
                copy.start()
                done_copies[p, q, b, t] = copy

    def summed(b, q, p):
        for t in (1, 3, 2):
            done_copies[p, q, b, t].wait_recv()
        totals = [jnp.zeros((WIDTH, 16, 128), F32) for _ in range(4)]
        for t in range(4):
            if t == 0:
                real, imag = ydone[p, q, yy, b, 0], ydone[p, q, yy, b, 1]
            else:
                real, imag = ydone_all[p, q, t, b, 0], ydone_all[p, q, t, b, 1]
            cosine, sine = trig[t, 0, b, q, planes(p)], trig[t, 1, b, q, planes(p)]
            coef = mill[lax.rem(yy + t, 4)]
            across = imag * cosine - real * sine
            totals[0] = totals[0] + real * cosine + imag * sine
            for c in range(3):
                totals[1 + c] = totals[1 + c] + coef[c : c + 1][None] * across
        return totals

    part_copies = {}
    for p in range(2):
        for b, q in ((1, 0), (1, 1), (0, 1), (0, 0)):
            for f, total in enumerate(summed(b, q, p)):
                part[b, q, p, f] = total
            if (b, q) != (0, 0):
                copy = remote(
                    part.at[b, q, p], part_recv.at[b, q, p], part_sem.at[b, q, p], across(b, q)
                )
                copy.start()
                part_copies[b, q, p] = copy

    for p in range(2):
        sums = [part[0, 0, p, f] for f in range(4)]
        for b, q in BLOCKS:
            part_copies[b, q, p].wait_recv()
            sums = [sums[f] + part_recv[b, q, p, f] for f in range(4)]
        mask = sup[planes(p)].astype(F32)
        amp_out[planes(p)] = mask * (sums[0] + lapped[0, planes(p)])
        for c in range(3):
            disp_out[c, planes(p)] = (
                own[0, planes(p)] * sums[1 + c] + lapped[1 + c, planes(p)]
            )

    for copy in (*mill_copies, *raw_copies.values(), *part_copies.values()):
        copy.wait_send()
    for there, copy in zip(has, edges):
        pl.when(there)(copy.wait_send)
    for at in obj_copies:
        obj_copies[at].wait_send()
        done_copies[at].wait_send()
    for h in range(2):
        for p in range(2):
            wait_sent(fwd_send, fwd_recv, slab_sem, h, p)
            wait_sent(back_send, back_recv, slab_back_sem, h, p)


def body(amplitude, displacement, support, miller, shift_kz, intensity):
    vmem = pl.BlockSpec(memory_space=pltpu.VMEM)
    smem = pl.BlockSpec(memory_space=pltpu.SMEM)
    anywhere = pl.BlockSpec(memory_space=pl.ANY)
    block = (ROWS, 16, 128)
    chunk = (WIDTH, 16, 128)
    sems = pltpu.SemaphoreType.DMA
    return pl.pallas_call(
        kernel,
        out_shape=(
            jax.ShapeDtypeStruct(block, F32),
            jax.ShapeDtypeStruct((3, *block), F32),
        ),
        in_specs=[vmem, vmem, anywhere, smem, smem, anywhere],
        out_specs=(vmem, vmem),
        scratch_shapes=[
            pltpu.VMEM(block, jnp.int32),
            pltpu.VMEM((2, 2048, 128), F32),
            pltpu.VMEM((2, 2, 4, *block), F32),
            pltpu.VMEM((4, 8, 128), F32),
            pltpu.VMEM((2, 16, 128), F32),
            pltpu.VMEM((2, 16, 128), F32),
            pltpu.VMEM((2, 4, 16, 128), F32),
            pltpu.VMEM((4, 2, 2, 2, *block), F32),
            pltpu.VMEM((4, 2, 2, 2, 2, *chunk), F32),
            pltpu.VMEM((2, 2, 4, 2, 2, *chunk), F32),
            pltpu.VMEM((2, 768, 256), BF16),
            pltpu.VMEM((2, 2, 2, LINES, 128), F32),
            pltpu.VMEM((2, 2, 2, LINES, 128), F32),
            pltpu.VMEM((2, 2, 2, LINES, 128), F32),
            pltpu.VMEM((2, 2, 2, LINES, 128), F32),
            pltpu.VMEM((2, 2, 4, 2, 2, *chunk), F32),
            pltpu.VMEM((2, 2, 4, 2, 2, *chunk), F32),
            pltpu.VMEM((2, 2, 2, 4, *chunk), F32),
            pltpu.VMEM((2, 2, 2, 4, *chunk), F32),
            pltpu.VMEM((4, *block), F32),
            pltpu.VMEM((256, 768), BF16),
            pltpu.VMEM((256, 768), BF16),
            pltpu.VMEM((512, 768), BF16),
            pltpu.VMEM((256, 1536), BF16),
            pltpu.VMEM((768, 512), BF16),
            pltpu.VMEM((1536, 256), BF16),
            sems((3,)),
            sems((2, 2, 2, 2)),
            sems((4, 2)),
            sems((4, 2)),
            sems((2, 2, 2, 4, 2)),
            sems((2, 2, 2, 4, 2)),
            sems((2, 2, 2)),
            sems((2, 2, 2)),
            sems((2, 2, 2, 2)),
        ],
        compiler_params=pltpu.CompilerParams(
            collective_id=0, has_side_effects=True, vmem_limit_bytes=56 * 1024 * 1024
        ),
        name="gradient",
    )(amplitude, displacement, support, miller, shift_kz, intensity.reshape(2048, 256))


def solution(mesh):
    placed = (
        P("slab", "refl", None),
        P(None, "slab", "refl", None),
        P("slab", None, None),
        P("refl", None),
        P("refl"),
        P("refl", None, "slab", None),
    )
    return jax.shard_map(
        body,
        mesh=mesh,
        in_specs=placed,
        out_specs=(P("slab", "refl", None), P(None, "slab", "refl", None)),
        check_vma=False,
    )
```

time: 89.3 us -> 85 us (0.952)
  Pallas kernels: 84.8 us -> 80.6 us
    pallas_call x1, Pallas kernels: 84.8 us -> 80.6 us  [body(): pl.pallas_call(kernel, out_shape=(jax.ShapeDtypeStruct(block, F32), jax.S...]
where the time goes in v4:
time: 85 us; the launch traced here: 84.8 us
  Pallas kernels  80.6 us (95%)
  local copies, waits for them, and re-layouts  2.91 us (3%)
  between operations  1.29 us (2%)
    pallas_call x1, Pallas kernels, body(): pl.pallas_call(kernel, out_shape=(jax.ShapeDtypeStruct(block, F32), jax.S...  80.6 us
    unnamed x2, local copies, waits for them, and re-layouts  2.91 us

profile of v4, /device:TPU:1, one launch (start us, length us, event | category | flops | bytes accessed | tf_op | source)
XLA Modules:
  0.0 84.8 jit_solution(11909793269456973678)
XLA Ops:
  1.3 80.6 %gradient.1 = (f32[4,16,128]{2,1,0:T(8,128)}, f32[3,4,16,128]{3,2,1,0:T(8,128)}) custom-call(f32[4,16,128]{2,1,0:T(8,128)} %amp_ref.1, f32[3,4,16,128]{3,2,1,0:T(8,128)} %disp_ref.1, s32[4,128,128]{2,1,0:T(8,128)} %sup_hbm.1, s32[1,3]{1,0:T(1,128)} %miller_ref.1, s32[1]{0:T(128)S(6)} %copy.10.shift_ref, f32[2048,256]{1,0:T(8,128)} %bitcast.1), custom_call_target="tpu_custom_call" | custom-call | tf_op jit(solution)/shard_map/gradient/pallas_call | solution.py:461
  81.9 1.4 %copy.11 = f32[4,16,128]{2,1,0:T(8,128)} copy(f32[4,16,128]{2,1,0:T(8,128)} %get-tuple-element.4) | data formatting | bytes 65536
  83.3 1.5 %copy.12 = f32[3,4,16,128]{3,2,1,0:T(8,128)} copy(f32[3,4,16,128]{3,2,1,0:T(8,128)} %get-tuple-element.5) | data formatting | bytes 196608

commit v5 on v4

--- a/solution.py
+++ b/solution.py
@@ -99,7 +99,7 @@
     amp_ref, disp_ref, sup_hbm, miller_ref, shift_ref, int_hbm,
     amp_out, disp_out,
     sup, inten, raw, mill, ey_send, ey_recv, ex_recv, trig, obj, obj_all, bcat,
-    fwd_send, fwd_recv, back_send, back_recv, ydone, ydone_all, part, part_recv, lapped,
+    fwd_send, fwd_recv, back_send, back_recv, ydone, ydone_all, part, part_own, part_recv, lapped,
     y_fwd, y_back, x_fwd, x_back, z_fwd, z_back,
     load_sem, raw_sem, mill_sem, edge_sem, peer_sem, peer_back_sem, slab_sem, slab_back_sem, part_sem,
 ):
@@ -218,6 +218,9 @@
     def freq_y(i):
         return 8 * (TEAM * team + ((i >> 1) & 15)) + 4 * (i >> 7) + ((i >> 5) & 3), i & 1
 
+    def freq_y_all(i):
+        return 8 * ((i >> 1) & 31) + 4 * (i >> 8) + ((i >> 6) & 3), i & 1
+
     def place_x(i):
         side = ((i >> 6) & 1) + team
         return 64 * (side & 1) + 4 * (i & 15) + 2 * ((i >> 5) & 1) + ((i >> 4) & 1), i >> 7
@@ -235,8 +238,9 @@
         weight, d0, d1, d2 = [raw[b, q, f, planes(p)] for f in range(4)]
         phase = m0 * d0 + m1 * d1 + m2 * d2
         cosine, sine = cos_sin_turns(phase * (1.0 / (2 * math.pi)) + turn)
-        trig[t, 0, b, q, planes(p)] = cosine
-        trig[t, 1, b, q, planes(p)] = sine
+        if q == 0:
+            trig[t, 0, b, planes(p)] = cosine
+            trig[t, 1, b, planes(p)] = sine
         ref[0] = weight * cosine
         ref[1] = weight * sine
 
@@ -259,31 +263,53 @@
             raw_copies[b, q, p].wait_recv()
             object_block(p, b, q)
 
-    def slab_sends(src, dst, sems, h, p):
+    def team_sends(h, p):
         def lines(i):
             return (h, p, slice(None), pl.ds(pl.multiple_of(lax.rem(i, TEAM) * 16, 16), 16))
 
         def send(j, carry):
             to = TEAM * team + lax.rem(me + j, TEAM)
             pltpu.make_async_remote_copy(
-                src_ref=src.at[lines(to)],
-                dst_ref=dst.at[lines(me)],
-                send_sem=sems.at[0, h, p],
-                recv_sem=sems.at[1, h, p],
+                src_ref=fwd_send.at[lines(to)],
+                dst_ref=fwd_recv.at[lines(me)],
+                send_sem=slab_sem.at[0, h, p],
+                recv_sem=slab_sem.at[1, h, p],
                 device_id={"slab": to},
                 device_id_type=MESH,
             ).start()
             return carry
 
         lax.fori_loop(1, TEAM, send, 0)
-        pltpu.make_async_copy(src.at[lines(me)], dst.at[lines(me)], sems.at[1, h, p]).start()
-
-    def wait_sent(src, dst, sems, h, p):
-        most = (h, p, slice(None), pl.ds(0, LINES - 16))
-        pltpu.make_async_copy(src.at[most], dst.at[most], sems.at[0, h, p]).wait()
-
-    def wait_arrived(dst, sems, h, p):
-        pltpu.make_async_copy(dst.at[h, p], dst.at[h, p], sems.at[1, h, p]).wait()
+        pltpu.make_async_copy(
+            fwd_send.at[lines(me)], fwd_recv.at[lines(me)], slab_sem.at[1, h, p]
+        ).start()
+
+    whole = slice(None)
+    back_groups = ((0, whole), (1, 0), (1, 1))
+
+    def slab_sends(g):
+        def lines(i):
+            return (*back_groups[g], pl.ds(pl.multiple_of(i * 16, 16), 16))
+
+        def send(j, carry):
+            to = lax.rem(me + j, SLABS)
+            pltpu.make_async_remote_copy(
+                src_ref=back_send.at[lines(to)],
+                dst_ref=back_recv.at[lines(me)],
+                send_sem=slab_back_sem.at[0, g],
+                recv_sem=slab_back_sem.at[1, g],
+                device_id={"slab": to},
+                device_id_type=MESH,
+            ).start()
+            return carry
+
+        lax.fori_loop(1, SLABS, send, 0)
+        pltpu.make_async_copy(
+            back_send.at[lines(me)], back_recv.at[lines(me)], slab_back_sem.at[1, g]
+        ).start()
+
+    def wait_all(ref, at, sem):
+        pltpu.make_async_copy(ref.at[at], ref.at[at], sem).wait()
 
     for p in range(2):
         for b, q in ((0, 0), *BLOCKS):
@@ -300,19 +326,19 @@
                         fwd_send[h, p, q, pl.ds(4 * j + k, 32, stride=8), :] = out[
                             32 * k : 32 * (k + 1), 128 * j : 128 * (j + 1)
                         ]
-            slab_sends(fwd_send, fwd_recv, slab_sem, h, p)
+            team_sends(h, p)
 
     fill_table(x_fwd, (512, 256), True, freq_plain, place_x, True)
     fill_table(z_fwd, (256, 512), False, freq_plain, place_plain, False)
     fill_table(x_back, (256, 512), False, freq_plain, place_x, True)
     fill_table(z_back, (512, 256), True, freq_plain, place_plain, False)
-    fill_table(y_back, (256, 256), False, freq_y, place_y, True)
+    fill_table(y_back, (256, 512), False, freq_y_all, place_y, True)
     for copy in int_copies:
         copy.wait()
 
     for h in range(2):
         for p in range(2):
-            wait_arrived(fwd_recv, slab_sem, h, p)
+            wait_all(fwd_recv, (h, p), slab_sem.at[1, h, p])
 
         def row(k, carry):
             sides = [
@@ -342,14 +368,15 @@
             for c in range(2):
                 for at in range(8):
                     q, p, j = at // 4, at // 2 % 2, at % 2
-                    back_send[h, p, q, pl.ds(c * 8 + 4 * j + k, 16, stride=16), :] = out[
+                    first = LINES * lax.rem(q + team, 2) + c * 8 + 4 * j + k
+                    back_send[h, p, pl.ds(first, 16, stride=16), :] = out[
                         16 * at : 16 * (at + 1), 128 * c : 128 * (c + 1)
                     ]
             return carry
 
         lax.fori_loop(0, 4, row, 0)
-        for p in range(2):
-            slab_sends(back_send, back_recv, slab_back_sem, h, p)
+        for g in ((0,), (1, 2))[h]:
+            slab_sends(g)
 
     for there, copy in ((has[0], up_y), (has[1], down_y), (has[2], up_x), (has[3], down_x)):
         pl.when(there)(copy.wait_recv)
@@ -369,44 +396,43 @@
 
     done_copies = {}
     for p in range(2):
-        for h in range(2):
-            wait_arrived(back_recv, slab_back_sem, h, p)
-        for q in range(2):
-            columns = [
-                jnp.concatenate(
-                    [
-                        back_recv[h, p, q, pl.ds(4 * j + k, 32, stride=8), :]
-                        for h in range(2)
-                        for k in range(4)
-                    ],
-                    axis=0,
-                )
-                for j in range(WIDTH)
-            ]
-            out = dot(y_back[...], stacked(jnp.concatenate(columns, axis=1)))
-            for j in range(WIDTH):
-                ydone[p, q, :, :, :, j] = out[:, 128 * j : 128 * (j + 1)].reshape(4, 2, 2, 16, 128)
-        for b, q in ((1, 0), (1, 1), (0, 1), (0, 0)):
+        for g in ((0, 1), (2,))[p]:
+            wait_all(back_recv, back_groups[g], slab_back_sem.at[1, g])
+        columns = [
+            jnp.concatenate(
+                [
+                    back_recv[h, p, pl.ds(4 * j + k, 64, stride=8), :]
+                    for h in range(2)
+                    for k in range(4)
+                ],
+                axis=0,
+            )
+            for j in range(WIDTH)
+        ]
+        out = dot(y_back[...], stacked(jnp.concatenate(columns, axis=1)))
+        for j in range(WIDTH):
+            ydone[p, :, :, :, j] = out[:, 128 * j : 128 * (j + 1)].reshape(4, 2, 2, 16, 128)
+        for b in (1, 0):
             for t in (2, 1, 3):
                 copy = remote(
-                    ydone.at[p, q, lax.rem(yy + t, 4), b],
-                    ydone_all.at[p, q, 4 - t, b],
-                    peer_back_sem.at[p, q, b, t],
+                    ydone.at[p, lax.rem(yy + t, 4), b],
+                    ydone_all.at[p, 4 - t, b],
+                    peer_back_sem.at[p, b, t],
                     peer_of(t),
                 )
                 copy.start()
-                done_copies[p, q, b, t] = copy
-
-    def summed(b, q, p):
+                done_copies[p, b, t] = copy
+
+    def summed(b, p):
         for t in (1, 3, 2):
-            done_copies[p, q, b, t].wait_recv()
+            done_copies[p, b, t].wait_recv()
         totals = [jnp.zeros((WIDTH, 16, 128), F32) for _ in range(4)]
         for t in range(4):
             if t == 0:
-                real, imag = ydone[p, q, yy, b, 0], ydone[p, q, yy, b, 1]
+                real, imag = ydone[p, yy, b, 0], ydone[p, yy, b, 1]
             else:
-                real, imag = ydone_all[p, q, t, b, 0], ydone_all[p, q, t, b, 1]
-            cosine, sine = trig[t, 0, b, q, planes(p)], trig[t, 1, b, q, planes(p)]
+                real, imag = ydone_all[p, t, b, 0], ydone_all[p, t, b, 1]
+            cosine, sine = trig[t, 0, b, planes(p)], trig[t, 1, b, planes(p)]
             coef = mill[lax.rem(yy + t, 4)]
             across = imag * cosine - real * sine
             totals[0] = totals[0] + real * cosine + imag * sine
@@ -414,41 +440,38 @@
                 totals[1 + c] = totals[1 + c] + coef[c : c + 1][None] * across
         return totals
 
-    part_copies = {}
-    for p in range(2):
-        for b, q in ((1, 0), (1, 1), (0, 1), (0, 0)):
-            for f, total in enumerate(summed(b, q, p)):
-                part[b, q, p, f] = total
-            if (b, q) != (0, 0):
-                copy = remote(
-                    part.at[b, q, p], part_recv.at[b, q, p], part_sem.at[b, q, p], across(b, q)
-                )
-                copy.start()
-                part_copies[b, q, p] = copy
-
-    for p in range(2):
-        sums = [part[0, 0, p, f] for f in range(4)]
-        for b, q in BLOCKS:
-            part_copies[b, q, p].wait_recv()
-            sums = [sums[f] + part_recv[b, q, p, f] for f in range(4)]
+    part_copies = []
+    for p in range(2):
+        for f, total in enumerate(summed(1, p)):
+            part[p, f] = total
+        copy = remote(part.at[p], part_recv.at[p], part_sem.at[p], across(1, 0))
+        copy.start()
+        part_copies.append(copy)
+    for p in range(2):
+        for f, total in enumerate(summed(0, p)):
+            part_own[p, f] = total
+
+    for p in range(2):
+        part_copies[p].wait_recv()
         mask = sup[planes(p)].astype(F32)
-        amp_out[planes(p)] = mask * (sums[0] + lapped[0, planes(p)])
+        amp_out[planes(p)] = mask * (part_own[p, 0] + part_recv[p, 0] + lapped[0, planes(p)])
         for c in range(3):
             disp_out[c, planes(p)] = (
-                own[0, planes(p)] * sums[1 + c] + lapped[1 + c, planes(p)]
+                own[0, planes(p)] * (part_own[p, 1 + c] + part_recv[p, 1 + c])
+                + lapped[1 + c, planes(p)]
             )
 
-    for copy in (*mill_copies, *raw_copies.values(), *part_copies.values()):
+    for copy in (*mill_copies, *raw_copies.values(), *part_copies):
         copy.wait_send()
     for there, copy in zip(has, edges):
         pl.when(there)(copy.wait_send)
-    for at in obj_copies:
-        obj_copies[at].wait_send()
-        done_copies[at].wait_send()
+    for copy in (*obj_copies.values(), *done_copies.values()):
+        copy.wait_send()
     for h in range(2):
         for p in range(2):
-            wait_sent(fwd_send, fwd_recv, slab_sem, h, p)
-            wait_sent(back_send, back_recv, slab_back_sem, h, p)
+            wait_all(fwd_send, (h, p, whole, pl.ds(0, LINES - 16)), slab_sem.at[0, h, p])
+    for g in range(3):
+        wait_all(back_send, (*back_groups[g], pl.ds(0, 2 * LINES - 16)), slab_back_sem.at[0, g])
 
 
 def body(amplitude, displacement, support, miller, shift_kz, intensity):
@@ -474,21 +497,22 @@
             pltpu.VMEM((2, 16, 128), F32),
             pltpu.VMEM((2, 16, 128), F32),
             pltpu.VMEM((2, 4, 16, 128), F32),
-            pltpu.VMEM((4, 2, 2, 2, *block), F32),
+            pltpu.VMEM((4, 2, 2, *block), F32),
             pltpu.VMEM((4, 2, 2, 2, 2, *chunk), F32),
             pltpu.VMEM((2, 2, 4, 2, 2, *chunk), F32),
             pltpu.VMEM((2, 768, 256), BF16),
             pltpu.VMEM((2, 2, 2, LINES, 128), F32),
             pltpu.VMEM((2, 2, 2, LINES, 128), F32),
-            pltpu.VMEM((2, 2, 2, LINES, 128), F32),
-            pltpu.VMEM((2, 2, 2, LINES, 128), F32),
-            pltpu.VMEM((2, 2, 4, 2, 2, *chunk), F32),
-            pltpu.VMEM((2, 2, 4, 2, 2, *chunk), F32),
-            pltpu.VMEM((2, 2, 2, 4, *chunk), F32),
-            pltpu.VMEM((2, 2, 2, 4, *chunk), F32),
+            pltpu.VMEM((2, 2, 2 * LINES, 128), F32),
+            pltpu.VMEM((2, 2, 2 * LINES, 128), F32),
+            pltpu.VMEM((2, 4, 2, 2, *chunk), F32),
+            pltpu.VMEM((2, 4, 2, 2, *chunk), F32),
+            pltpu.VMEM((2, 4, *chunk), F32),
+            pltpu.VMEM((2, 4, *chunk), F32),
+            pltpu.VMEM((2, 4, *chunk), F32),
             pltpu.VMEM((4, *block), F32),
             pltpu.VMEM((256, 768), BF16),
-            pltpu.VMEM((256, 768), BF16),
+            pltpu.VMEM((256, 1536), BF16),
             pltpu.VMEM((512, 768), BF16),
             pltpu.VMEM((256, 1536), BF16),
             pltpu.VMEM((768, 512), BF16),
@@ -498,10 +522,10 @@
             sems((4, 2)),
             sems((4, 2)),
             sems((2, 2, 2, 4, 2)),
-            sems((2, 2, 2, 4, 2)),
+            sems((2, 2, 4, 2)),
             sems((2, 2, 2)),
-            sems((2, 2, 2)),
-            sems((2, 2, 2, 2)),
+            sems((2, 3)),
+            sems((2, 2)),
         ],
         compiler_params=pltpu.CompilerParams(
             collective_id=0, has_side_effects=True, vmem_limit_bytes=56 * 1024 * 1024

time: 85 us -> 86.7 us (1.020)
  the two profiles are of different devices: /device:TPU:1 before, /device:TPU:38 now
where the time goes in v5:
time: 86.7 us; the launch traced here: 86.4 us
  Pallas kernels  82.2 us (95%)
  local copies, waits for them, and re-layouts  2.91 us (3%)
  between operations  1.29 us (1%)
    pallas_call x1, Pallas kernels, body(): pl.pallas_call(kernel, out_shape=(jax.ShapeDtypeStruct(block, F32), jax.S...  82.2 us
    unnamed x2, local copies, waits for them, and re-layouts  2.91 us

profile of v5, /device:TPU:38, one launch (start us, length us, event | category | flops | bytes accessed | tf_op | source)
XLA Modules:
  0.0 86.4 jit_solution(550576186953005198)
XLA Ops:
  1.3 82.2 %gradient.1 = (f32[4,16,128]{2,1,0:T(8,128)}, f32[3,4,16,128]{3,2,1,0:T(8,128)}) custom-call(f32[4,16,128]{2,1,0:T(8,128)} %amp_ref.1, f32[3,4,16,128]{3,2,1,0:T(8,128)} %disp_ref.1, s32[4,128,128]{2,1,0:T(8,128)} %sup_hbm.1, s32[1,3]{1,0:T(1,128)} %miller_ref.1, s32[1]{0:T(128)S(6)} %copy.10.shift_ref, f32[2048,256]{1,0:T(8,128)} %bitcast.1), custom_call_target="tpu_custom_call" | custom-call | tf_op jit(solution)/shard_map/gradient/pallas_call | solution.py:484
  83.5 1.4 %copy.11 = f32[4,16,128]{2,1,0:T(8,128)} copy(f32[4,16,128]{2,1,0:T(8,128)} %get-tuple-element.4) | data formatting | bytes 65536
  84.9 1.5 %copy.12 = f32[3,4,16,128]{3,2,1,0:T(8,128)} copy(f32[3,4,16,128]{3,2,1,0:T(8,128)} %get-tuple-element.5) | data formatting | bytes 196608

commit v6 on v4

--- a/solution.py
+++ b/solution.py
@@ -17,6 +17,7 @@
 WIDTH = 2
 TEAM = SLABS // 2
 LINES = TEAM * 16
+UNROLL = 4
 BLOCKS = ((0, 1), (1, 1), (1, 0))
 
 
@@ -99,7 +100,7 @@
     amp_ref, disp_ref, sup_hbm, miller_ref, shift_ref, int_hbm,
     amp_out, disp_out,
     sup, inten, raw, mill, ey_send, ey_recv, ex_recv, trig, obj, obj_all, bcat,
-    fwd_send, fwd_recv, back_send, back_recv, ydone, ydone_all, part, part_recv, lapped,
+    fwd_send, fwd_recv, zed, zedb, back_send, back_recv, ydone, ydone_all, part, part_recv, lapped,
     y_fwd, y_back, x_fwd, x_back, z_fwd, z_back,
     load_sem, raw_sem, mill_sem, edge_sem, peer_sem, peer_back_sem, slab_sem, slab_back_sem, part_sem,
 ):
@@ -188,6 +189,7 @@
         for p in range(2)
         for b, q in BLOCKS
     }
+
     mill_copies = [
         remote(mill.at[yy], mill.at[yy], mill_sem.at[t], peer_of(t)) for t in (1, 2, 3)
     ]
@@ -314,22 +316,25 @@
         for p in range(2):
             wait_arrived(fwd_recv, slab_sem, h, p)
 
+        sides = [
+            jnp.concatenate(
+                [
+                    fwd_recv[h, p, q, pl.ds(c * 8 + 4 * j + k, 16, stride=16), :]
+                    for k in range(4)
+                    for q in range(2)
+                    for p in range(2)
+                    for j in range(WIDTH)
+                ],
+                axis=0,
+            )
+            for c in range(2)
+        ]
+        zed[...] = dot(abreast(jnp.concatenate(sides, axis=1)), z_fwd[...])
+
         def row(k, carry):
-            sides = [
-                jnp.concatenate(
-                    [
-                        fwd_recv[h, p, q, pl.ds(c * 8 + 4 * j + k, 16, stride=16), :]
-                        for q in range(2)
-                        for p in range(2)
-                        for j in range(WIDTH)
-                    ],
-                    axis=0,
-                )
-                for c in range(2)
-            ]
-            zed = dot(abreast(jnp.concatenate(sides, axis=1)), z_fwd[...])
+            lines = pl.ds(pl.multiple_of(128 * k, 128), 128)
             spec = dot(
-                x_fwd[...], stacked(jnp.concatenate([zed[:, :256], zed[:, 256:]], axis=0))
+                x_fwd[...], stacked(jnp.concatenate([zed[lines, :256], zed[lines, 256:]], axis=0))
             )
             real, imag = spec[:256], spec[256:]
             measured = jnp.concatenate(
@@ -338,16 +343,23 @@
             excess = 4.0 * (real * real + imag * imag - measured)
             residual = jnp.concatenate([excess * real, excess * imag], axis=0)
             back = dot(x_back[...], stacked(residual))
-            out = dot(abreast(jnp.concatenate([back[:128], back[128:]], axis=1)), z_back[...])
+            for c in range(2):
+                high, low = split(back[128 * c : 128 * (c + 1)])
+                zedb[lines, 256 * c : 256 * (c + 1)] = high
+                zedb[lines, 512 + 256 * c : 512 + 256 * (c + 1)] = low
+                zedb[lines, 1024 + 256 * c : 1024 + 256 * (c + 1)] = high
+            return carry
+
+        lax.fori_loop(0, 4, row, 0, unroll=UNROLL)
+        out = dot(zedb[...], z_back[...])
+        for k in range(4):
             for c in range(2):
                 for at in range(8):
                     q, p, j = at // 4, at // 2 % 2, at % 2
+                    first = 128 * k + 16 * at
                     back_send[h, p, q, pl.ds(c * 8 + 4 * j + k, 16, stride=16), :] = out[
-                        16 * at : 16 * (at + 1), 128 * c : 128 * (c + 1)
+                        first : first + 16, 128 * c : 128 * (c + 1)
                     ]
-            return carry
-
-        lax.fori_loop(0, 4, row, 0)
         for p in range(2):
             slab_sends(back_send, back_recv, slab_back_sem, h, p)
 
@@ -368,6 +380,18 @@
         lapped[f] = 2.0 * (EDGE_WEIGHT if f == 0 else STRAIN_WEIGHT) * (6.0 * x - beside)
 
     done_copies = {}
+
+    def done_send(p, q, b):
+        for t in (2, 1, 3):
+            copy = remote(
+                ydone.at[p, q, lax.rem(yy + t, 4), b],
+                ydone_all.at[p, q, 4 - t, b],
+                peer_back_sem.at[p, q, b, t],
+                peer_of(t),
+            )
+            copy.start()
+            done_copies[p, q, b, t] = copy
+
     for p in range(2):
         for h in range(2):
             wait_arrived(back_recv, slab_back_sem, h, p)
@@ -386,16 +410,10 @@
             out = dot(y_back[...], stacked(jnp.concatenate(columns, axis=1)))
             for j in range(WIDTH):
                 ydone[p, q, :, :, :, j] = out[:, 128 * j : 128 * (j + 1)].reshape(4, 2, 2, 16, 128)
-        for b, q in ((1, 0), (1, 1), (0, 1), (0, 0)):
-            for t in (2, 1, 3):
-                copy = remote(
-                    ydone.at[p, q, lax.rem(yy + t, 4), b],
-                    ydone_all.at[p, q, 4 - t, b],
-                    peer_back_sem.at[p, q, b, t],
-                    peer_of(t),
-                )
-                copy.start()
-                done_copies[p, q, b, t] = copy
+        for b, q in ((1, 0), (1, 1), (0, 1)):
+            done_send(p, q, b)
+    for p in range(2):
+        done_send(p, 0, 0)
 
     def summed(b, q, p):
         for t in (1, 3, 2):
@@ -416,18 +434,17 @@
 
     part_copies = {}
     for p in range(2):
-        for b, q in ((1, 0), (1, 1), (0, 1), (0, 0)):
+        for b, q in ((1, 0), (1, 1), (0, 1)):
             for f, total in enumerate(summed(b, q, p)):
                 part[b, q, p, f] = total
-            if (b, q) != (0, 0):
-                copy = remote(
-                    part.at[b, q, p], part_recv.at[b, q, p], part_sem.at[b, q, p], across(b, q)
-                )
-                copy.start()
-                part_copies[b, q, p] = copy
-
-    for p in range(2):
-        sums = [part[0, 0, p, f] for f in range(4)]
+            copy = remote(
+                part.at[b, q, p], part_recv.at[b, q, p], part_sem.at[b, q, p], across(b, q)
+            )
+            copy.start()
+            part_copies[b, q, p] = copy
+
+    for p in range(2):
+        sums = summed(0, 0, p)
         for b, q in BLOCKS:
             part_copies[b, q, p].wait_recv()
             sums = [sums[f] + part_recv[b, q, p, f] for f in range(4)]
@@ -480,6 +497,8 @@
             pltpu.VMEM((2, 768, 256), BF16),
             pltpu.VMEM((2, 2, 2, LINES, 128), F32),
             pltpu.VMEM((2, 2, 2, LINES, 128), F32),
+            pltpu.VMEM((512, 512), F32),
+            pltpu.VMEM((512, 1536), BF16),
             pltpu.VMEM((2, 2, 2, LINES, 128), F32),
             pltpu.VMEM((2, 2, 2, LINES, 128), F32),
             pltpu.VMEM((2, 2, 4, 2, 2, *chunk), F32),

time: 85 us -> 80.6 us (0.948)
  Pallas kernels: 80.6 us -> 76.1 us
    pallas_call x1, Pallas kernels: 80.6 us -> 76.1 us  [body(): pl.pallas_call(kernel, out_shape=(jax.ShapeDtypeStruct(block, F32), jax.S...]
where the time goes in v6:
time: 80.6 us; the launch traced here: 80.3 us
  Pallas kernels  76.1 us (94%)
  local copies, waits for them, and re-layouts  2.91 us (4%)
  between operations  1.29 us (2%)
    pallas_call x1, Pallas kernels, body(): pl.pallas_call(kernel, out_shape=(jax.ShapeDtypeStruct(block, F32), jax.S...  76.1 us
    unnamed x2, local copies, waits for them, and re-layouts  2.91 us

profile of v6, /device:TPU:1, one launch (start us, length us, event | category | flops | bytes accessed | tf_op | source)
XLA Modules:
  0.0 80.3 jit_solution(17661934603352963727)
XLA Ops:
  1.3 76.1 %gradient.1 = (f32[4,16,128]{2,1,0:T(8,128)}, f32[3,4,16,128]{3,2,1,0:T(8,128)}) custom-call(f32[4,16,128]{2,1,0:T(8,128)} %amp_ref.1, f32[3,4,16,128]{3,2,1,0:T(8,128)} %disp_ref.1, s32[4,128,128]{2,1,0:T(8,128)} %sup_hbm.1, s32[1,3]{1,0:T(1,128)} %miller_ref.1, s32[1]{0:T(128)S(6)} %copy.10.shift_ref, f32[2048,256]{1,0:T(8,128)} %bitcast.1), custom_call_target="tpu_custom_call" | custom-call | tf_op jit(solution)/shard_map/gradient/pallas_call | solution.py:478
  77.4 1.4 %copy.11 = f32[4,16,128]{2,1,0:T(8,128)} copy(f32[4,16,128]{2,1,0:T(8,128)} %get-tuple-element.4) | data formatting | bytes 65536
  78.8 1.5 %copy.12 = f32[3,4,16,128]{3,2,1,0:T(8,128)} copy(f32[3,4,16,128]{3,2,1,0:T(8,128)} %get-tuple-element.5) | data formatting | bytes 196608

commit v7 on v6

--- a/solution.py
+++ b/solution.py
@@ -16,8 +16,8 @@
 ROWS = 4
 WIDTH = 2
 TEAM = SLABS // 2
-LINES = TEAM * 16
-UNROLL = 4
+GROUPS = 4
+LINES = TEAM * 8
 BLOCKS = ((0, 1), (1, 1), (1, 0))
 
 
@@ -97,9 +97,9 @@
 
 
 def kernel(
-    amp_ref, disp_ref, sup_hbm, miller_ref, shift_ref, int_hbm,
+    amp_hbm, disp_hbm, sup_hbm, miller_hbm, shift_hbm, int_hbm,
     amp_out, disp_out,
-    sup, inten, raw, mill, ey_send, ey_recv, ex_recv, trig, obj, obj_all, bcat,
+    amp, miller_ref, shift_ref, sup, inten, raw, mill, ey_send, ey_recv, ex_recv, trig, obj, obj_all, bcat,
     fwd_send, fwd_recv, zed, zedb, back_send, back_recv, ydone, ydone_all, part, part_recv, lapped,
     y_fwd, y_back, x_fwd, x_back, z_fwd, z_back,
     load_sem, raw_sem, mill_sem, edge_sem, peer_sem, peer_back_sem, slab_sem, slab_back_sem, part_sem,
@@ -120,13 +120,19 @@
     sup_copy = pltpu.make_async_copy(
         sup_hbm.at[:, pl.ds(pl.multiple_of(refl * 16, 16), 16), :], sup, load_sem.at[0]
     )
-    sup_copy.start()
+    first_copies = [
+        pltpu.make_async_copy(miller_hbm, miller_ref, load_sem.at[3]),
+        pltpu.make_async_copy(shift_hbm, shift_ref, load_sem.at[4]),
+        sup_copy,
+        pltpu.make_async_copy(amp_hbm, amp, load_sem.at[5]),
+        pltpu.make_async_copy(disp_hbm, own.at[pl.ds(1, 3)], load_sem.at[6]),
+    ]
+    for copy in first_copies:
+        copy.start()
     int_copies = [
         pltpu.make_async_copy(int_hbm.at[:, pl.ds(128 * j, 128)], inten.at[j], load_sem.at[1 + j])
         for j in range(2)
     ]
-    for copy in int_copies:
-        copy.start()
 
     barrier = pltpu.get_barrier_semaphore()
 
@@ -146,7 +152,10 @@
     lax.fori_loop(1, SLABS, greet_slab, 0)
     pl.semaphore_signal(barrier, inc=1, device_id=across(1, 1), device_id_type=MESH)
 
-    own[1:4] = disp_ref[...]
+    for copy in first_copies:
+        copy.wait()
+    for copy in int_copies:
+        copy.start()
     lane_row = lax.broadcasted_iota(jnp.int32, (8, 128), 0)
     tile = jnp.where(
         lane_row == 0,
@@ -158,9 +167,8 @@
         ),
     )
     mill[yy] = tile
-    sup_copy.wait()
     mask = sup[...].astype(F32)
-    own[0] = mask * amp_ref[...]
+    own[0] = mask * amp[...]
     for f in range(4):
         for x in range(ROWS):
             at = f * 4 + x
@@ -261,31 +269,35 @@
             raw_copies[b, q, p].wait_recv()
             object_block(p, b, q)
 
-    def slab_sends(src, dst, sems, h, p):
+    whole = slice(None)
+    fwd_groups = ((whole, 0), (0, 1), (1, 1), (2, 1), (3, 1))
+    back_groups = ((0, whole), (1, whole), (2, whole), (3, 0), (3, 1))
+
+    def slab_sends(src, dst, sems, at, g):
         def lines(i):
-            return (h, p, slice(None), pl.ds(pl.multiple_of(lax.rem(i, TEAM) * 16, 16), 16))
+            return (*at, whole, pl.ds(pl.multiple_of(lax.rem(i, TEAM) * 8, 8), 8))
 
         def send(j, carry):
             to = TEAM * team + lax.rem(me + j, TEAM)
             pltpu.make_async_remote_copy(
                 src_ref=src.at[lines(to)],
                 dst_ref=dst.at[lines(me)],
-                send_sem=sems.at[0, h, p],
-                recv_sem=sems.at[1, h, p],
+                send_sem=sems.at[0, g],
+                recv_sem=sems.at[1, g],
                 device_id={"slab": to},
                 device_id_type=MESH,
             ).start()
             return carry
 
         lax.fori_loop(1, TEAM, send, 0)
-        pltpu.make_async_copy(src.at[lines(me)], dst.at[lines(me)], sems.at[1, h, p]).start()
-
-    def wait_sent(src, dst, sems, h, p):
-        most = (h, p, slice(None), pl.ds(0, LINES - 16))
-        pltpu.make_async_copy(src.at[most], dst.at[most], sems.at[0, h, p]).wait()
-
-    def wait_arrived(dst, sems, h, p):
-        pltpu.make_async_copy(dst.at[h, p], dst.at[h, p], sems.at[1, h, p]).wait()
+        pltpu.make_async_copy(src.at[lines(me)], dst.at[lines(me)], sems.at[1, g]).start()
+
+    def wait_sent(src, dst, sems, at, g):
+        most = (*at, whole, pl.ds(0, LINES - 8))
+        pltpu.make_async_copy(src.at[most], dst.at[most], sems.at[0, g]).wait()
+
+    def wait_arrived(dst, sems, at, g):
+        pltpu.make_async_copy(dst.at[at], dst.at[at], sems.at[1, g]).wait()
 
     for p in range(2):
         for b, q in ((0, 0), *BLOCKS):
@@ -299,10 +311,14 @@
                 out = dot(y_fwd[128 * h : 128 * (h + 1), :], bcat[q])
                 for k in range(4):
                     for j in range(WIDTH):
-                        fwd_send[h, p, q, pl.ds(4 * j + k, 32, stride=8), :] = out[
+                        fwd_send[2 * h + k // 2, p, q, pl.ds(2 * j + k % 2, 32, stride=4), :] = out[
                             32 * k : 32 * (k + 1), 128 * j : 128 * (j + 1)
                         ]
-            slab_sends(fwd_send, fwd_recv, slab_sem, h, p)
+            if p == 1:
+                for g in (2 * h + 1, 2 * h + 2):
+                    slab_sends(fwd_send, fwd_recv, slab_sem, fwd_groups[g], g)
+        if p == 0:
+            slab_sends(fwd_send, fwd_recv, slab_sem, fwd_groups[0], 0)
 
     fill_table(x_fwd, (512, 256), True, freq_plain, place_x, True)
     fill_table(z_fwd, (256, 512), False, freq_plain, place_plain, False)
@@ -312,15 +328,14 @@
     for copy in int_copies:
         copy.wait()
 
-    for h in range(2):
-        for p in range(2):
-            wait_arrived(fwd_recv, slab_sem, h, p)
-
+    wait_arrived(fwd_recv, slab_sem, fwd_groups[0], 0)
+    for h in range(GROUPS):
+        wait_arrived(fwd_recv, slab_sem, fwd_groups[1 + h], 1 + h)
         sides = [
             jnp.concatenate(
                 [
-                    fwd_recv[h, p, q, pl.ds(c * 8 + 4 * j + k, 16, stride=16), :]
-                    for k in range(4)
+                    fwd_recv[h, p, q, pl.ds(c * 4 + 2 * j + k, 16, stride=8), :]
+                    for k in range(2)
                     for q in range(2)
                     for p in range(2)
                     for j in range(WIDTH)
@@ -329,39 +344,38 @@
             )
             for c in range(2)
         ]
-        zed[...] = dot(abreast(jnp.concatenate(sides, axis=1)), z_fwd[...])
-
-        def row(k, carry):
-            lines = pl.ds(pl.multiple_of(128 * k, 128), 128)
+        zed[h % 2] = dot(abreast(jnp.concatenate(sides, axis=1)), z_fwd[...])
+        for k in range(2):
+            lines = slice(128 * k, 128 * (k + 1))
             spec = dot(
-                x_fwd[...], stacked(jnp.concatenate([zed[lines, :256], zed[lines, 256:]], axis=0))
+                x_fwd[...],
+                stacked(
+                    jnp.concatenate([zed[h % 2, lines, :256], zed[h % 2, lines, 256:]], axis=0)
+                ),
             )
             real, imag = spec[:256], spec[256:]
             measured = jnp.concatenate(
-                [inten[j, pl.ds(4 * h + k, 256, stride=8), :] for j in range(2)], axis=1
+                [inten[j, pl.ds(2 * h + k, 256, stride=8), :] for j in range(2)], axis=1
             )
             excess = 4.0 * (real * real + imag * imag - measured)
             residual = jnp.concatenate([excess * real, excess * imag], axis=0)
             back = dot(x_back[...], stacked(residual))
             for c in range(2):
                 high, low = split(back[128 * c : 128 * (c + 1)])
-                zedb[lines, 256 * c : 256 * (c + 1)] = high
-                zedb[lines, 512 + 256 * c : 512 + 256 * (c + 1)] = low
-                zedb[lines, 1024 + 256 * c : 1024 + 256 * (c + 1)] = high
-            return carry
-
-        lax.fori_loop(0, 4, row, 0, unroll=UNROLL)
-        out = dot(zedb[...], z_back[...])
-        for k in range(4):
+                zedb[h % 2, lines, 256 * c : 256 * (c + 1)] = high
+                zedb[h % 2, lines, 512 + 256 * c : 512 + 256 * (c + 1)] = low
+                zedb[h % 2, lines, 1024 + 256 * c : 1024 + 256 * (c + 1)] = high
+        out = dot(zedb[h % 2], z_back[...])
+        for k in range(2):
             for c in range(2):
                 for at in range(8):
                     q, p, j = at // 4, at // 2 % 2, at % 2
                     first = 128 * k + 16 * at
-                    back_send[h, p, q, pl.ds(c * 8 + 4 * j + k, 16, stride=16), :] = out[
+                    back_send[h, p, q, pl.ds(c * 4 + 2 * j + k, 16, stride=8), :] = out[
                         first : first + 16, 128 * c : 128 * (c + 1)
                     ]
-        for p in range(2):
-            slab_sends(back_send, back_recv, slab_back_sem, h, p)
+        for g in (h,) if h < GROUPS - 1 else (h, h + 1):
+            slab_sends(back_send, back_recv, slab_back_sem, back_groups[g], g)
 
     for there, copy in ((has[0], up_y), (has[1], down_y), (has[2], up_x), (has[3], down_x)):
         pl.when(there)(copy.wait_recv)
@@ -393,15 +407,15 @@
             done_copies[p, q, b, t] = copy
 
     for p in range(2):
-        for h in range(2):
-            wait_arrived(back_recv, slab_back_sem, h, p)
+        for g in ((0, 1, 2, 3), (4,))[p]:
+            wait_arrived(back_recv, slab_back_sem, back_groups[g], g)
         for q in range(2):
             columns = [
                 jnp.concatenate(
                     [
-                        back_recv[h, p, q, pl.ds(4 * j + k, 32, stride=8), :]
-                        for h in range(2)
-                        for k in range(4)
+                        back_recv[h, p, q, pl.ds(2 * j + k, 32, stride=4), :]
+                        for h in range(GROUPS)
+                        for k in range(2)
                     ],
                     axis=0,
                 )
@@ -462,15 +476,13 @@
     for at in obj_copies:
         obj_copies[at].wait_send()
         done_copies[at].wait_send()
-    for h in range(2):
-        for p in range(2):
-            wait_sent(fwd_send, fwd_recv, slab_sem, h, p)
-            wait_sent(back_send, back_recv, slab_back_sem, h, p)
+    for g in range(GROUPS + 1):
+        wait_sent(fwd_send, fwd_recv, slab_sem, fwd_groups[g], g)
+        wait_sent(back_send, back_recv, slab_back_sem, back_groups[g], g)
 
 
 def body(amplitude, displacement, support, miller, shift_kz, intensity):
     vmem = pl.BlockSpec(memory_space=pltpu.VMEM)
-    smem = pl.BlockSpec(memory_space=pltpu.SMEM)
     anywhere = pl.BlockSpec(memory_space=pl.ANY)
     block = (ROWS, 16, 128)
     chunk = (WIDTH, 16, 128)
@@ -481,9 +493,12 @@
             jax.ShapeDtypeStruct(block, F32),
             jax.ShapeDtypeStruct((3, *block), F32),
         ),
-        in_specs=[vmem, vmem, anywhere, smem, smem, anywhere],
+        in_specs=[anywhere] * 6,
         out_specs=(vmem, vmem),
         scratch_shapes=[
+            pltpu.VMEM(block, F32),
+            pltpu.SMEM((1, 3), jnp.int32),
+            pltpu.SMEM((1,), jnp.int32),
             pltpu.VMEM(block, jnp.int32),
             pltpu.VMEM((2, 2048, 128), F32),
             pltpu.VMEM((2, 2, 4, *block), F32),
@@ -495,12 +510,12 @@
             pltpu.VMEM((4, 2, 2, 2, 2, *chunk), F32),
             pltpu.VMEM((2, 2, 4, 2, 2, *chunk), F32),
             pltpu.VMEM((2, 768, 256), BF16),
-            pltpu.VMEM((2, 2, 2, LINES, 128), F32),
-            pltpu.VMEM((2, 2, 2, LINES, 128), F32),
-            pltpu.VMEM((512, 512), F32),
-            pltpu.VMEM((512, 1536), BF16),
-            pltpu.VMEM((2, 2, 2, LINES, 128), F32),
-            pltpu.VMEM((2, 2, 2, LINES, 128), F32),
+            pltpu.VMEM((GROUPS, 2, 2, LINES, 128), F32),
+            pltpu.VMEM((GROUPS, 2, 2, LINES, 128), F32),
+            pltpu.VMEM((2, 256, 512), F32),
+            pltpu.VMEM((2, 256, 1536), BF16),
+            pltpu.VMEM((GROUPS, 2, 2, LINES, 128), F32),
+            pltpu.VMEM((GROUPS, 2, 2, LINES, 128), F32),
             pltpu.VMEM((2, 2, 4, 2, 2, *chunk), F32),
             pltpu.VMEM((2, 2, 4, 2, 2, *chunk), F32),
             pltpu.VMEM((2, 2, 2, 4, *chunk), F32),
@@ -512,14 +527,14 @@
             pltpu.VMEM((256, 1536), BF16),
             pltpu.VMEM((768, 512), BF16),
             pltpu.VMEM((1536, 256), BF16),
-            sems((3,)),
+            sems((7,)),
             sems((2, 2, 2, 2)),
             sems((4, 2)),
             sems((4, 2)),
             sems((2, 2, 2, 4, 2)),
             sems((2, 2, 2, 4, 2)),
-            sems((2, 2, 2)),
-            sems((2, 2, 2)),
+            sems((2, GROUPS + 1)),
+            sems((2, GROUPS + 1)),
             sems((2, 2, 2, 2)),
         ],
         compiler_params=pltpu.CompilerParams(

time: 80.6 us -> 79.9 us (level)
  no operation moved by 1% of the time
where the time goes in v7:
time: 79.9 us; the launch traced here: 79.6 us
  Pallas kernels  75.4 us (94%)
  local copies, waits for them, and re-layouts  2.91 us (4%)
  between operations  1.29 us (2%)
    pallas_call x1, Pallas kernels, body(): pl.pallas_call(kernel, out_shape=(jax.ShapeDtypeStruct(block, F32), jax.S...  75.4 us
    unnamed x2, local copies, waits for them, and re-layouts  2.91 us

profile of v7, /device:TPU:1, one launch (start us, length us, event | category | flops | bytes accessed | tf_op | source)
XLA Modules:
  0.0 79.6 jit_solution(14327086843450815856)
XLA Ops:
  1.3 75.4 %gradient.1 = (f32[4,16,128]{2,1,0:T(8,128)}, f32[3,4,16,128]{3,2,1,0:T(8,128)}) custom-call(f32[4,16,128]{2,1,0:T(8,128)} %amp_hbm.1, f32[3,4,16,128]{3,2,1,0:T(8,128)} %disp_hbm.1, s32[4,128,128]{2,1,0:T(8,128)} %sup_hbm.1, s32[1,3]{1,0:T(1,128)} %miller_hbm.1, s32[1]{0:T(128)S(6)} %copy.10.shift_hbm, f32[2048,256]{1,0:T(8,128)} %bitcast.1), custom_call_target="tpu_custom_call" | custom-call | tf_op jit(solution)/shard_map/gradient/pallas_call | solution.py:490
  76.7 1.4 %copy.11 = f32[4,16,128]{2,1,0:T(8,128)} copy(f32[4,16,128]{2,1,0:T(8,128)} %get-tuple-element.4) | data formatting | bytes 65536
  78.1 1.5 %copy.12 = f32[3,4,16,128]{3,2,1,0:T(8,128)} copy(f32[3,4,16,128]{3,2,1,0:T(8,128)} %get-tuple-element.5) | data formatting | bytes 196608

commit v8 on v7

--- a/solution.py
+++ b/solution.py
@@ -100,9 +100,9 @@
     amp_hbm, disp_hbm, sup_hbm, miller_hbm, shift_hbm, int_hbm,
     amp_out, disp_out,
     amp, miller_ref, shift_ref, sup, inten, raw, mill, ey_send, ey_recv, ex_recv, trig, obj, obj_all, bcat,
-    fwd_send, fwd_recv, zed, zedb, back_send, back_recv, ydone, ydone_all, part, part_recv, lapped,
-    y_fwd, y_back, x_fwd, x_back, z_fwd, z_back,
-    load_sem, raw_sem, mill_sem, edge_sem, peer_sem, peer_back_sem, slab_sem, slab_back_sem, part_sem,
+    fwd_send, fwd_recv, zed, zedb, back_send, back_recv, owner_send, owner_recv, ydone, ydone_all, part, part_recv, lapped,
+    y_fwd, y_back, y_back_all, x_fwd, x_back, z_fwd, z_back,
+    load_sem, raw_sem, mill_sem, edge_sem, peer_sem, peer_back_sem, slab_sem, slab_back_sem, owner_sem, part_sem,
 ):
     refl = lax.axis_index("refl")
     me = lax.axis_index("slab")
@@ -228,6 +228,9 @@
     def freq_y(i):
         return 8 * (TEAM * team + ((i >> 1) & 15)) + 4 * (i >> 7) + ((i >> 5) & 3), i & 1
 
+    def freq_y_all(i):
+        return 8 * ((i >> 1) & 31) + 2 * (i >> 7) + ((i >> 6) & 1), i & 1
+
     def place_x(i):
         side = ((i >> 6) & 1) + team
         return 64 * (side & 1) + 4 * (i & 15) + 2 * ((i >> 5) & 1) + ((i >> 4) & 1), i >> 7
@@ -271,7 +274,7 @@
 
     whole = slice(None)
     fwd_groups = ((whole, 0), (0, 1), (1, 1), (2, 1), (3, 1))
-    back_groups = ((0, whole), (1, whole), (2, whole), (3, 0), (3, 1))
+    halves = (pl.ds(0, 2), pl.ds(2, 2))
 
     def slab_sends(src, dst, sems, at, g):
         def lines(i):
@@ -291,6 +294,27 @@
 
         lax.fori_loop(1, TEAM, send, 0)
         pltpu.make_async_copy(src.at[lines(me)], dst.at[lines(me)], sems.at[1, g]).start()
+
+    def owner_sends(g):
+        def lines(i):
+            return (halves[g], pl.ds(pl.multiple_of(i * 8, 8), 8))
+
+        def send(j, carry):
+            to = lax.rem(me + j, SLABS)
+            pltpu.make_async_remote_copy(
+                src_ref=owner_send.at[lines(to)],
+                dst_ref=owner_recv.at[lines(me)],
+                send_sem=owner_sem.at[0, g],
+                recv_sem=owner_sem.at[1, g],
+                device_id={"slab": to},
+                device_id_type=MESH,
+            ).start()
+            return carry
+
+        lax.fori_loop(1, SLABS, send, 0)
+        pltpu.make_async_copy(
+            owner_send.at[lines(me)], owner_recv.at[lines(me)], owner_sem.at[1, g]
+        ).start()
 
     def wait_sent(src, dst, sems, at, g):
         most = (*at, whole, pl.ds(0, LINES - 8))
@@ -325,6 +349,7 @@
     fill_table(x_back, (256, 512), False, freq_plain, place_x, True)
     fill_table(z_back, (512, 256), True, freq_plain, place_plain, False)
     fill_table(y_back, (256, 256), False, freq_y, place_y, True)
+    fill_table(y_back_all, (256, 512), False, freq_y_all, place_y, True)
     for copy in int_copies:
         copy.wait()
 
@@ -371,11 +396,16 @@
                 for at in range(8):
                     q, p, j = at // 4, at // 2 % 2, at % 2
                     first = 128 * k + 16 * at
-                    back_send[h, p, q, pl.ds(c * 4 + 2 * j + k, 16, stride=8), :] = out[
-                        first : first + 16, 128 * c : 128 * (c + 1)
-                    ]
-        for g in (h,) if h < GROUPS - 1 else (h, h + 1):
-            slab_sends(back_send, back_recv, slab_back_sem, back_groups[g], g)
+                    value = out[first : first + 16, 128 * c : 128 * (c + 1)]
+                    line = c * 4 + 2 * j + k
+                    if p == 0:
+                        back_send[h, q, pl.ds(line, 16, stride=8), :] = value
+                    else:
+                        line = LINES * lax.rem(q + team, 2) + line
+                        owner_send[h, pl.ds(line, 16, stride=8), :] = value
+        slab_sends(back_send, back_recv, slab_back_sem, (h,), h)
+        if h % 2 == 1:
+            owner_sends(h // 2)
 
     for there, copy in ((has[0], up_y), (has[1], down_y), (has[2], up_x), (has[3], down_x)):
         pl.when(there)(copy.wait_recv)
@@ -406,28 +436,31 @@
             copy.start()
             done_copies[p, q, b, t] = copy
 
-    for p in range(2):
-        for g in ((0, 1, 2, 3), (4,))[p]:
-            wait_arrived(back_recv, slab_back_sem, back_groups[g], g)
-        for q in range(2):
-            columns = [
-                jnp.concatenate(
-                    [
-                        back_recv[h, p, q, pl.ds(2 * j + k, 32, stride=4), :]
-                        for h in range(GROUPS)
-                        for k in range(2)
-                    ],
-                    axis=0,
-                )
-                for j in range(WIDTH)
-            ]
-            out = dot(y_back[...], stacked(jnp.concatenate(columns, axis=1)))
-            for j in range(WIDTH):
-                ydone[p, q, :, :, :, j] = out[:, 128 * j : 128 * (j + 1)].reshape(4, 2, 2, 16, 128)
-        for b, q in ((1, 0), (1, 1), (0, 1)):
-            done_send(p, q, b)
-    for p in range(2):
-        done_send(p, 0, 0)
+    def why_back(p, q, table, load):
+        columns = [
+            jnp.concatenate(
+                [load(h, 2 * j + k) for h in range(GROUPS) for k in range(2)], axis=0
+            )
+            for j in range(WIDTH)
+        ]
+        out = dot(table[...], stacked(jnp.concatenate(columns, axis=1)))
+        for j in range(WIDTH):
+            ydone[p, q, :, :, :, j] = out[:, 128 * j : 128 * (j + 1)].reshape(4, 2, 2, 16, 128)
+
+    for g in range(GROUPS):
+        wait_arrived(back_recv, slab_back_sem, (g,), g)
+    for q in range(2):
+        why_back(0, q, y_back, lambda h, line: back_recv[h, q, pl.ds(line, 32, stride=4), :])
+    for b, q in ((1, 0), (1, 1), (0, 1)):
+        done_send(0, q, b)
+    for g in range(2):
+        pltpu.make_async_copy(
+            owner_recv.at[halves[g]], owner_recv.at[halves[g]], owner_sem.at[1, g]
+        ).wait()
+    why_back(1, 0, y_back_all, lambda h, line: owner_recv[h, pl.ds(line, 64, stride=4), :])
+    done_send(1, 0, 1)
+    done_send(0, 0, 0)
+    done_send(1, 0, 0)
 
     def summed(b, q, p):
         for t in (1, 3, 2):
@@ -447,19 +480,16 @@
         return totals
 
     part_copies = {}
-    for p in range(2):
-        for b, q in ((1, 0), (1, 1), (0, 1)):
-            for f, total in enumerate(summed(b, q, p)):
-                part[b, q, p, f] = total
-            copy = remote(
-                part.at[b, q, p], part_recv.at[b, q, p], part_sem.at[b, q, p], across(b, q)
-            )
-            copy.start()
-            part_copies[b, q, p] = copy
+    for b, q, p in ((1, 0, 0), (1, 1, 0), (0, 1, 0), (1, 0, 1)):
+        for f, total in enumerate(summed(b, q, p)):
+            part[b, q, p, f] = total
+        copy = remote(part.at[b, q, p], part_recv.at[b, q, p], part_sem.at[b, q, p], across(b, q))
+        copy.start()
+        part_copies[b, q, p] = copy
 
     for p in range(2):
         sums = summed(0, 0, p)
-        for b, q in BLOCKS:
+        for b, q in BLOCKS if p == 0 else BLOCKS[2:]:
             part_copies[b, q, p].wait_recv()
             sums = [sums[f] + part_recv[b, q, p, f] for f in range(4)]
         mask = sup[planes(p)].astype(F32)
@@ -473,12 +503,15 @@
         copy.wait_send()
     for there, copy in zip(has, edges):
         pl.when(there)(copy.wait_send)
-    for at in obj_copies:
-        obj_copies[at].wait_send()
-        done_copies[at].wait_send()
+    for copy in (*obj_copies.values(), *done_copies.values()):
+        copy.wait_send()
     for g in range(GROUPS + 1):
         wait_sent(fwd_send, fwd_recv, slab_sem, fwd_groups[g], g)
-        wait_sent(back_send, back_recv, slab_back_sem, back_groups[g], g)
+    for g in range(GROUPS):
+        wait_sent(back_send, back_recv, slab_back_sem, (g,), g)
+    for g in range(2):
+        most = (halves[g], pl.ds(0, 2 * LINES - 8))
+        pltpu.make_async_copy(owner_send.at[most], owner_recv.at[most], owner_sem.at[0, g]).wait()
 
 
 def body(amplitude, displacement, support, miller, shift_kz, intensity):
@@ -514,8 +547,10 @@
             pltpu.VMEM((GROUPS, 2, 2, LINES, 128), F32),
             pltpu.VMEM((2, 256, 512), F32),
             pltpu.VMEM((2, 256, 1536), BF16),
-            pltpu.VMEM((GROUPS, 2, 2, LINES, 128), F32),
-            pltpu.VMEM((GROUPS, 2, 2, LINES, 128), F32),
+            pltpu.VMEM((GROUPS, 2, LINES, 128), F32),
+            pltpu.VMEM((GROUPS, 2, LINES, 128), F32),
+            pltpu.VMEM((GROUPS, 2 * LINES, 128), F32),
+            pltpu.VMEM((GROUPS, 2 * LINES, 128), F32),
             pltpu.VMEM((2, 2, 4, 2, 2, *chunk), F32),
             pltpu.VMEM((2, 2, 4, 2, 2, *chunk), F32),
             pltpu.VMEM((2, 2, 2, 4, *chunk), F32),
@@ -523,6 +558,7 @@
             pltpu.VMEM((4, *block), F32),
             pltpu.VMEM((256, 768), BF16),
             pltpu.VMEM((256, 768), BF16),
+            pltpu.VMEM((256, 1536), BF16),
             pltpu.VMEM((512, 768), BF16),
             pltpu.VMEM((256, 1536), BF16),
             pltpu.VMEM((768, 512), BF16),
@@ -534,7 +570,8 @@
             sems((2, 2, 2, 4, 2)),
             sems((2, 2, 2, 4, 2)),
             sems((2, GROUPS + 1)),
-            sems((2, GROUPS + 1)),
+            sems((2, GROUPS)),
+            sems((2, 2)),
             sems((2, 2, 2, 2)),
         ],
         compiler_params=pltpu.CompilerParams(

time: 79.9 us -> 78.5 us (0.982)
  Pallas kernels: 75.4 us -> 74.1 us
    pallas_call x1, Pallas kernels: 75.4 us -> 74.1 us  [body(): pl.pallas_call(kernel, out_shape=(jax.ShapeDtypeStruct(block, F32), jax.S...]
where the time goes in v8:
time: 78.5 us; the launch traced here: 78.3 us
  Pallas kernels  74.1 us (94%)
  local copies, waits for them, and re-layouts  2.91 us (4%)
  between operations  1.29 us (2%)
    pallas_call x1, Pallas kernels, body(): pl.pallas_call(kernel, out_shape=(jax.ShapeDtypeStruct(block, F32), jax.S...  74.1 us
    unnamed x2, local copies, waits for them, and re-layouts  2.91 us

profile of v8, /device:TPU:1, one launch (start us, length us, event | category | flops | bytes accessed | tf_op | source)
XLA Modules:
  0.0 78.3 jit_solution(16187355937393670560)
XLA Ops:
  1.3 74.1 %gradient.1 = (f32[4,16,128]{2,1,0:T(8,128)}, f32[3,4,16,128]{3,2,1,0:T(8,128)}) custom-call(f32[4,16,128]{2,1,0:T(8,128)} %amp_hbm.1, f32[3,4,16,128]{3,2,1,0:T(8,128)} %disp_hbm.1, s32[4,128,128]{2,1,0:T(8,128)} %sup_hbm.1, s32[1,3]{1,0:T(1,128)} %miller_hbm.1, s32[1]{0:T(128)S(6)} %copy.10.shift_hbm, f32[2048,256]{1,0:T(8,128)} %bitcast.1), custom_call_target="tpu_custom_call" | custom-call | tf_op jit(solution)/shard_map/gradient/pallas_call | solution.py:523
  75.4 1.4 %copy.11 = f32[4,16,128]{2,1,0:T(8,128)} copy(f32[4,16,128]{2,1,0:T(8,128)} %get-tuple-element.4) | data formatting | bytes 65536
  76.8 1.5 %copy.12 = f32[3,4,16,128]{3,2,1,0:T(8,128)} copy(f32[3,4,16,128]{3,2,1,0:T(8,128)} %get-tuple-element.5) | data formatting | bytes 196608

commit v9 on v8

--- a/solution.py
+++ b/solution.py
@@ -267,6 +267,9 @@
 
     for p in range(2):
         object_block(p, 0, 0)
+    fill_table(x_fwd, (512, 256), True, freq_plain, place_x, True)
+    fill_table(z_fwd, (256, 512), False, freq_plain, place_plain, False)
+    fill_table(x_back, (256, 512), False, freq_plain, place_x, True)
     for p in range(2):
         for b, q in BLOCKS:
             raw_copies[b, q, p].wait_recv()
@@ -344,9 +347,6 @@
         if p == 0:
             slab_sends(fwd_send, fwd_recv, slab_sem, fwd_groups[0], 0)
 
-    fill_table(x_fwd, (512, 256), True, freq_plain, place_x, True)
-    fill_table(z_fwd, (256, 512), False, freq_plain, place_plain, False)
-    fill_table(x_back, (256, 512), False, freq_plain, place_x, True)
     fill_table(z_back, (512, 256), True, freq_plain, place_plain, False)
     fill_table(y_back, (256, 256), False, freq_y, place_y, True)
     fill_table(y_back_all, (256, 512), False, freq_y_all, place_y, True)
@@ -453,13 +453,13 @@
         why_back(0, q, y_back, lambda h, line: back_recv[h, q, pl.ds(line, 32, stride=4), :])
     for b, q in ((1, 0), (1, 1), (0, 1)):
         done_send(0, q, b)
+    done_send(0, 0, 0)
     for g in range(2):
         pltpu.make_async_copy(
             owner_recv.at[halves[g]], owner_recv.at[halves[g]], owner_sem.at[1, g]
         ).wait()
     why_back(1, 0, y_back_all, lambda h, line: owner_recv[h, pl.ds(line, 64, stride=4), :])
     done_send(1, 0, 1)
-    done_send(0, 0, 0)
     done_send(1, 0, 0)
 
     def summed(b, q, p):

time: 78.5 us -> 78.3 us (level)
  the two profiles are of different devices: /device:TPU:1 before, /device:TPU:8 now
where the time goes in v9:
time: 78.3 us; the launch traced here: 78.1 us
  Pallas kernels  73.9 us (94%)
  local copies, waits for them, and re-layouts  2.91 us (4%)
  between operations  1.29 us (2%)
    pallas_call x1, Pallas kernels, body(): pl.pallas_call(kernel, out_shape=(jax.ShapeDtypeStruct(block, F32), jax.S...  73.9 us
    unnamed x2, local copies, waits for them, and re-layouts  2.91 us

profile of v9, /device:TPU:8, one launch (start us, length us, event | category | flops | bytes accessed | tf_op | source)
XLA Modules:
  0.0 78.1 jit_solution(1195083900087075844)
XLA Ops:
  1.3 73.9 %gradient.1 = (f32[4,16,128]{2,1,0:T(8,128)}, f32[3,4,16,128]{3,2,1,0:T(8,128)}) custom-call(f32[4,16,128]{2,1,0:T(8,128)} %amp_hbm.1, f32[3,4,16,128]{3,2,1,0:T(8,128)} %disp_hbm.1, s32[4,128,128]{2,1,0:T(8,128)} %sup_hbm.1, s32[1,3]{1,0:T(1,128)} %miller_hbm.1, s32[1]{0:T(128)S(6)} %copy.10.shift_hbm, f32[2048,256]{1,0:T(8,128)} %bitcast.1), custom_call_target="tpu_custom_call" | custom-call | tf_op jit(solution)/shard_map/gradient/pallas_call | solution.py:523
  75.2 1.4 %copy.11 = f32[4,16,128]{2,1,0:T(8,128)} copy(f32[4,16,128]{2,1,0:T(8,128)} %get-tuple-element.4) | data formatting | bytes 65536
  76.6 1.5 %copy.12 = f32[3,4,16,128]{3,2,1,0:T(8,128)} copy(f32[3,4,16,128]{3,2,1,0:T(8,128)} %get-tuple-element.5) | data formatting | bytes 196608
